TPU v7x, 32 devices: a whole 2x2x4 slice. The times are simulated.
32 devices in a mesh: dp: 4 (over y, x), ctx: 2 (over core), tp: 4 (over z).
Axes of the slice: x: 2, y: 2, z: 4, core: 2. Of those that a mesh axis runs over, the one named last changes fastest.
Arguments:
- tokens: bfloat16 [4, 512, 1024], P('dp', 'ctx'), may hold values from -6 to 6
- segments: int32 [4, 512], P('dp'), may hold values from 0 to 2, never falling along the last dimension, each value on 1 to 384 neighbouring positions
- cotangent: bfloat16 [4, 512, 1024], P('dp', 'ctx'), may hold values from -6 to 6
- mixer_gain: bfloat16 [1024], P(('dp', 'ctx')), may hold values from 0.5 to 1.5
- mlp_gain: bfloat16 [1024], P(('dp', 'ctx')), may hold values from 0.5 to 1.5
- query_weight: bfloat16 [1024, 1024], P(('dp', 'ctx'), 'tp'), may hold values from -0.1875 to 0.1875
- key_weight: bfloat16 [1024, 1024], P(('dp', 'ctx'), 'tp'), may hold values from -0.1875 to 0.1875
- value_weight: bfloat16 [1024, 2048], P(('dp', 'ctx'), 'tp'), may hold values from -0.1875 to 0.1875
- gate_weight: bfloat16 [1024, 2048], P(('dp', 'ctx'), 'tp'), may hold values from -0.1875 to 0.1875
- decay_weight: bfloat16 [1024, 8], P(('dp', 'ctx'), 'tp'), may hold values from -0.1875 to 0.1875
- beta_weight: bfloat16 [1024, 8], P(('dp', 'ctx'), 'tp'), may hold values from -0.1875 to 0.1875
- output_weight: bfloat16 [1024, 2048], P(('dp', 'ctx'), 'tp'), may hold values from -0.125 to 0.125
- conv_query: float32 [4, 1024], P(None, 'tp'), may hold values from -3 to 3
- conv_key: float32 [4, 1024], P(None, 'tp'), may hold values from -3 to 3
- conv_value: float32 [4, 2048], P(None, 'tp'), may hold values from -3 to 3
- decay_log: float32 [8], P('tp'), may hold values from -7 to -3
- decay_bias: float32 [8], P('tp'), may hold values from -2 to 1
- head_gain: float32 [256], replicated, may hold values from 0.5 to 1.5
- hidden_gate: bfloat16 [1024, 2816], P(('dp', 'ctx'), 'tp'), may hold values from -0.1875 to 0.1875
- hidden_up: bfloat16 [1024, 2816], P(('dp', 'ctx'), 'tp'), may hold values from -0.1875 to 0.1875
- hidden_down: bfloat16 [1024, 2816], P(('dp', 'ctx'), 'tp'), may hold values from -0.109375 to 0.109375
Outputs:
- block_out: bfloat16 [4, 512, 1024], P('dp', 'ctx')
- tokens_grad: float32 [4, 512, 1024], P('dp', 'ctx')
- mixer_gain_grad: float32 [1024], P(('dp', 'ctx'))
- mlp_gain_grad: float32 [1024], P(('dp', 'ctx'))
- query_grad: float32 [1024, 1024], P(('dp', 'ctx'), 'tp')
- key_grad: float32 [1024, 1024], P(('dp', 'ctx'), 'tp')
- value_grad: float32 [1024, 2048], P(('dp', 'ctx'), 'tp')
- gate_grad: float32 [1024, 2048], P(('dp', 'ctx'), 'tp')
- decay_grad: float32 [1024, 8], P(('dp', 'ctx'), 'tp')
- beta_grad: float32 [1024, 8], P(('dp', 'ctx'), 'tp')
- output_grad: float32 [1024, 2048], P(('dp', 'ctx'), 'tp')
- conv_query_grad: float32 [4, 1024], P(None, 'tp')
- conv_key_grad: float32 [4, 1024], P(None, 'tp')
- conv_value_grad: float32 [4, 2048], P(None, 'tp')
- decay_log_grad: float32 [8], P('tp')
- decay_bias_grad: float32 [8], P('tp')
- head_gain_grad: float32 [256], replicated
- hidden_gate_grad: float32 [1024, 2816], P(('dp', 'ctx'), 'tp')
- hidden_up_grad: float32 [1024, 2816], P(('dp', 'ctx'), 'tp')
- hidden_down_grad: float32 [1024, 2816], P(('dp', 'ctx'), 'tp')
Inputs may be any that keep to these rules, and one draw needn't show every extreme that they name: `segments`: along each sequence the numbers start at 0, never fall and rise by one at each document's first token; every document has 1 to 384 tokens and one has exactly 384.
All inputs are finite; a program needn't handle non-finite values.
Results may differ from a plain program's by a relative error of at most 0.014.
The roundings to bfloat16 on the way count: a program that leaves them out, or rounds other values in their place, can miss the bound.
Values may be sent and summed in bfloat16 or wider, within the bound.
A program may use at most 128 MiB of HBM per device.

v0:
```python
from functools import partial

import jax
import jax.numpy as jnp
from jax import lax
from jax.sharding import PartitionSpec as P

GROUP = 64


EPSILON = 1e-06
HIGHEST = lax.Precision.HIGHEST


def passed_along(value, axis, by):
    devices = lax.axis_size(axis)
    pairs = [(i, i + by) for i in range(devices) if 0 <= i + by < devices]
    return lax.ppermute(value, axis, pairs)


def features(pre_ext, seg_ext, conv_weight, decay_lin, beta_lin, decay_log, decay_bias, key_dim):
    margin = conv_weight.shape[0] - 1
    row_count = pre_ext.shape[0] - margin
    head_count = decay_lin.shape[1]
    own_segment = seg_ext[margin:]
    convolved = jnp.zeros((row_count, pre_ext.shape[1]), jnp.float32)
    for lag in range(margin + 1):
        first_row = margin - lag
        same_doc = (seg_ext[first_row : first_row + row_count] == own_segment).astype(jnp.float32)
        convolved = (
            convolved
            + conv_weight[lag][None, :]
            * pre_ext[first_row : first_row + row_count]
            * same_doc[:, None]
        )
    activated = jax.nn.silu(convolved)
    query_cols = head_count * key_dim
    queries = activated[:, :query_cols].reshape(row_count, head_count, key_dim)
    key_rows = activated[:, query_cols : 2 * query_cols].reshape(row_count, head_count, key_dim)
    value_rows = activated[:, 2 * query_cols :].reshape(row_count, head_count, -1)
    queries = (
        queries
        * lax.rsqrt(jnp.sum(queries * queries, -1, keepdims=True) + EPSILON)
        * key_dim ** (-0.5)
    )
    key_rows = key_rows * lax.rsqrt(jnp.sum(key_rows * key_rows, -1, keepdims=True) + EPSILON)
    decay_rate = -jnp.exp(decay_log)[None, :] * jax.nn.softplus(decay_lin + decay_bias[None, :])
    beta_gate = jax.nn.sigmoid(beta_lin)
    starts = (own_segment != seg_ext[margin - 1 : margin - 1 + row_count]).astype(jnp.float32)
    return (queries, key_rows, value_rows, decay_rate, beta_gate, starts)


def unit_lower_inverse(lower_part):
    order = lower_part.shape[-1]
    negated = -lower_part
    inverse = jnp.eye(order, dtype=jnp.float32)[None] + negated
    power = negated
    span = 2
    while span < order:
        power = jnp.einsum("hij,hjk->hik", power, power, precision=HIGHEST)
        inverse = inverse + jnp.einsum("hij,hjk->hik", inverse, power, precision=HIGHEST)
        span = span * 2
    return inverse


def group_update(memory, inputs):
    queries, key_rows, value_rows, decay_rate, beta_gate, starts = inputs
    order = queries.shape[0]
    cumulative = jnp.cumsum(decay_rate, axis=0)
    counted = jnp.cumsum(starts)
    position = jnp.arange(order)
    same_doc = (counted[:, None] == counted[None, :]) & (position[None, :] <= position[:, None])
    strictly = (same_doc & (position[None, :] < position[:, None])).astype(jnp.float32)
    spread = cumulative[:, None, :] - cumulative[None, :, :]
    decay_pair = (
        jnp.exp(jnp.where(same_doc[:, :, None], spread, 0.0))
        * same_doc.astype(jnp.float32)[:, :, None]
    )
    anchor = jnp.exp(cumulative) * (counted == 0).astype(jnp.float32)[:, None]
    closing = decay_pair[order - 1]
    key_gram = jnp.einsum("thd,jhd->htj", key_rows, key_rows, precision=HIGHEST)
    lower_part = (
        jnp.transpose(beta_gate)[:, :, None]
        * jnp.transpose(decay_pair, (2, 0, 1))
        * key_gram
        * strictly[None]
    )
    inverse = unit_lower_inverse(lower_part)
    key_state = jnp.einsum("thd,hdw->thw", key_rows, memory, precision=HIGHEST)
    target = beta_gate[:, :, None] * (value_rows - anchor[:, :, None] * key_state)
    updates = jnp.einsum("htj,jhw->thw", inverse, target, precision=HIGHEST)
    query_state = jnp.einsum("thd,hdw->thw", queries, memory, precision=HIGHEST)
    query_key = jnp.einsum("thd,jhd->tjh", queries, key_rows, precision=HIGHEST) * decay_pair
    output_rows = anchor[:, :, None] * query_state + jnp.einsum(
        "tjh,jhw->thw", query_key, updates, precision=HIGHEST
    )
    new_memory = anchor[order - 1][:, None, None] * memory + jnp.einsum(
        "jhd,jhw->hdw", key_rows * closing[:, :, None], updates, precision=HIGHEST
    )
    return (new_memory, output_rows)


def delta_run(queries, key_rows, value_rows, decay_rate, beta_gate, starts, memory, group):
    row_count = queries.shape[0]
    blocks = row_count // group
    pieces = tuple(
        (
            member.reshape((blocks, group) + member.shape[1:])
            for member in (queries, key_rows, value_rows, decay_rate, beta_gate, starts)
        )
    )
    last_memory, outputs = lax.scan(group_update, memory, pieces)
    return (last_memory, outputs.reshape((row_count,) + outputs.shape[2:]))


def gated(output_rows, gate_lin, head_gain):
    row_count, head_count, value_dim = output_rows.shape
    scaled = output_rows * lax.rsqrt(
        jnp.mean(output_rows * output_rows, -1, keepdims=True) + EPSILON
    )
    gate_rows = gate_lin.reshape(row_count, head_count, value_dim)
    return (scaled * head_gain * jax.nn.silu(gate_rows)).reshape(row_count, head_count * value_dim)


def expand(
    pre_ext, decay_lin, beta_lin, conv_weight, decay_log, decay_bias, seg_ext, key_dim, group
):
    queries, key_rows, value_rows, decay_rate, beta_gate, starts = features(
        pre_ext, seg_ext, conv_weight, decay_lin, beta_lin, decay_log, decay_bias, key_dim
    )
    row_count, head_count = decay_lin.shape
    value_dim = value_rows.shape[2]
    identity_rows = jnp.broadcast_to(
        jnp.eye(key_dim, dtype=jnp.float32), (head_count, key_dim, key_dim)
    )
    memory = jnp.concatenate(
        [identity_rows, jnp.zeros((head_count, key_dim, value_dim), jnp.float32)], 2
    )
    widened = jnp.concatenate(
        [jnp.zeros((row_count, head_count, key_dim), jnp.float32), value_rows], 2
    )
    last_memory, output_rows = delta_run(
        queries, key_rows, widened, decay_rate, beta_gate, starts, memory, group
    )
    return (
        output_rows[:, :, :key_dim],
        output_rows[:, :, key_dim:],
        last_memory[:, :, :key_dim],
        last_memory[:, :, key_dim:],
    )


def finish(carried, local_out, initial, gate_lin, head_gain):
    output_rows = local_out + jnp.einsum("thd,hdw->thw", carried, initial, precision=HIGHEST)
    return gated(output_rows, gate_lin, head_gain)


def apply_map(matrix, addend, incoming):
    return jnp.einsum("hde,hew->hdw", matrix, incoming, precision=HIGHEST) + addend


def local(
    tokens,
    segments,
    cotangent,
    mixer_gain,
    mlp_gain,
    query_weight,
    key_weight,
    value_weight,
    gate_weight,
    decay_weight,
    beta_weight,
    output_weight,
    conv_query,
    conv_key,
    conv_value,
    decay_log,
    decay_bias,
    head_gain,
    hidden_gate,
    hidden_up,
    hidden_down,
):
    width = tokens.shape[-1]
    inputs = tokens.reshape(-1, width).astype(jnp.float32)
    row_count = inputs.shape[0]
    gathered = (
        lax.all_gather(mixer_gain, ("dp", "ctx"), axis=0, tiled=True),
        lax.all_gather(mlp_gain, ("dp", "ctx"), axis=0, tiled=True),
        lax.all_gather(query_weight, ("dp", "ctx"), axis=0, tiled=True),
        lax.all_gather(key_weight, ("dp", "ctx"), axis=0, tiled=True),
        lax.all_gather(value_weight, ("dp", "ctx"), axis=0, tiled=True),
        lax.all_gather(gate_weight, ("dp", "ctx"), axis=0, tiled=True),
        lax.all_gather(decay_weight, ("dp", "ctx"), axis=0, tiled=True),
        lax.all_gather(beta_weight, ("dp", "ctx"), axis=0, tiled=True),
        lax.all_gather(output_weight, ("dp", "ctx"), axis=0, tiled=True),
        lax.all_gather(hidden_gate, ("dp", "ctx"), axis=0, tiled=True),
        lax.all_gather(hidden_up, ("dp", "ctx"), axis=0, tiled=True),
        lax.all_gather(hidden_down, ("dp", "ctx"), axis=0, tiled=True),
    )
    gain_one = gathered[0].astype(jnp.float32)
    gain_two = gathered[1].astype(jnp.float32)
    in_weights = jnp.concatenate(list(gathered[2:8]), 1)
    full_output = gathered[8]
    full_hidden_gate = gathered[9]
    full_hidden_up = gathered[10]
    full_hidden_down = gathered[11]
    query_cols = gathered[2].shape[1]
    value_cols = gathered[4].shape[1]
    head_count = gathered[6].shape[1]
    conv_cols = 2 * query_cols + value_cols
    key_dim = query_cols // head_count
    rms_one = lax.rsqrt(jnp.mean(inputs * inputs, -1, keepdims=True) + EPSILON)
    normed_one = inputs * rms_one
    hidden_one = (normed_one * gain_one).astype(jnp.bfloat16)
    projected = jnp.dot(hidden_one, in_weights, preferred_element_type=jnp.float32)
    pre_conv = projected[:, :conv_cols].astype(jnp.bfloat16)
    gate_lin = projected[:, conv_cols : conv_cols + value_cols]
    decay_lin = projected[:, conv_cols + value_cols : conv_cols + value_cols + head_count]
    beta_lin = projected[:, conv_cols + value_cols + head_count :]
    conv_weight = jnp.concatenate([conv_query, conv_key, conv_value], 1)
    margin = conv_weight.shape[0] - 1
    edge_rows = passed_along(pre_conv[row_count - margin :], "ctx", 1)
    pre_ext = jnp.concatenate([edge_rows, pre_conv], 0).astype(jnp.float32)
    seg_padded = jnp.concatenate([jnp.full((margin,), -1, jnp.int32), segments.reshape(-1)], 0)
    seg_ext = lax.dynamic_slice_in_dim(
        seg_padded, lax.axis_index("ctx") * row_count, row_count + margin
    )
    expand_fn = partial(expand, seg_ext=seg_ext, key_dim=key_dim, group=GROUP)
    (carried, local_out, transfer, offset), expand_back = jax.vjp(
        expand_fn, pre_ext, decay_lin, beta_lin, conv_weight, decay_log, decay_bias
    )

    def advance(turn, incoming):
        return passed_along(apply_map(transfer, offset, incoming), "ctx", 1)

    initial = lax.fori_loop(0, lax.axis_size("ctx") - 1, advance, jnp.zeros_like(offset))
    mixed, finish_back = jax.vjp(finish, carried, local_out, initial, gate_lin, head_gain)
    mixed_b = mixed.astype(jnp.bfloat16)
    mixer_part = jnp.einsum("rc,dc->rd", mixed_b, full_output, preferred_element_type=jnp.float32)
    attention = lax.psum(mixer_part, "tp")
    middle = inputs + attention
    rms_two = lax.rsqrt(jnp.mean(middle * middle, -1, keepdims=True) + EPSILON)
    normed_two = middle * rms_two
    hidden_two = (normed_two * gain_two).astype(jnp.bfloat16)
    gate_pre = jnp.dot(hidden_two, full_hidden_gate, preferred_element_type=jnp.float32)
    up_pre = jnp.dot(hidden_two, full_hidden_up, preferred_element_type=jnp.float32)
    sigma = jax.nn.sigmoid(gate_pre)
    swish = gate_pre * sigma
    activ = (swish * up_pre).astype(jnp.bfloat16)
    feed_part = jnp.einsum("rf,df->rd", activ, full_hidden_down, preferred_element_type=jnp.float32)
    feed = lax.psum(feed_part.astype(jnp.bfloat16), "tp").astype(jnp.float32)
    block_out = (middle + feed).astype(jnp.bfloat16).reshape(tokens.shape)
    regathered = (
        lax.all_gather(mixer_gain, ("dp", "ctx"), axis=0, tiled=True),
        lax.all_gather(mlp_gain, ("dp", "ctx"), axis=0, tiled=True),
        lax.all_gather(query_weight, ("dp", "ctx"), axis=0, tiled=True),
        lax.all_gather(key_weight, ("dp", "ctx"), axis=0, tiled=True),
        lax.all_gather(value_weight, ("dp", "ctx"), axis=0, tiled=True),
        lax.all_gather(gate_weight, ("dp", "ctx"), axis=0, tiled=True),
        lax.all_gather(decay_weight, ("dp", "ctx"), axis=0, tiled=True),
        lax.all_gather(beta_weight, ("dp", "ctx"), axis=0, tiled=True),
        lax.all_gather(output_weight, ("dp", "ctx"), axis=0, tiled=True),
        lax.all_gather(hidden_gate, ("dp", "ctx"), axis=0, tiled=True),
        lax.all_gather(hidden_up, ("dp", "ctx"), axis=0, tiled=True),
        lax.all_gather(hidden_down, ("dp", "ctx"), axis=0, tiled=True),
    )
    back_input = jnp.concatenate(list(regathered[2:8]), 1)
    back_output = regathered[8]
    back_gate = regathered[9]
    back_up = regathered[10]
    back_down = regathered[11]
    grad_rows = cotangent.reshape(-1, width)
    grad_out = grad_rows.astype(jnp.float32)
    d_activ = jnp.dot(grad_rows, back_down, preferred_element_type=jnp.float32)
    d_gate_pre = (d_activ * up_pre * sigma * (1.0 + gate_pre * (1.0 - sigma))).astype(jnp.bfloat16)
    d_up_pre = (d_activ * swish).astype(jnp.bfloat16)
    grad_down = jnp.einsum("rd,rf->df", grad_rows, activ, preferred_element_type=jnp.float32)
    grad_hgate = jnp.einsum("rd,rf->df", hidden_two, d_gate_pre, preferred_element_type=jnp.float32)
    grad_hup = jnp.einsum("rd,rf->df", hidden_two, d_up_pre, preferred_element_type=jnp.float32)
    two_part = jnp.einsum(
        "rf,df->rd", d_gate_pre, back_gate, preferred_element_type=jnp.float32
    ) + jnp.einsum("rf,df->rd", d_up_pre, back_up, preferred_element_type=jnp.float32)
    d_hidden_two = lax.psum(two_part, "tp")
    grad_gain_two = jnp.sum(d_hidden_two * normed_two, 0)
    dn_two = d_hidden_two * gain_two
    d_middle = grad_out + rms_two * (
        dn_two - normed_two * jnp.mean(dn_two * normed_two, -1, keepdims=True)
    )
    d_middle_b = d_middle.astype(jnp.bfloat16)
    d_mixed = jnp.dot(d_middle_b, back_output, preferred_element_type=jnp.float32)
    grad_output = jnp.einsum("rd,rc->dc", d_middle_b, mixed_b, preferred_element_type=jnp.float32)
    d_carried, d_local, init_grad, d_gate, d_head = finish_back(d_mixed)
    transposed = jnp.transpose(transfer, (0, 2, 1))

    def retreat(turn, outgoing):
        return passed_along(apply_map(transposed, init_grad, outgoing), "ctx", -1)

    end_grad = lax.fori_loop(0, lax.axis_size("ctx") - 1, retreat, jnp.zeros_like(offset))
    d_transfer = jnp.einsum("hdw,hew->hde", end_grad, initial, precision=HIGHEST)
    d_pre_ext, d_decay, d_beta, d_conv, d_log, d_bias = expand_back(
        (d_carried, d_local, d_transfer, end_grad)
    )
    edge_back = passed_along(d_pre_ext[:margin], "ctx", -1)
    own_grad = d_pre_ext[margin:]
    d_pre = jnp.concatenate(
        [own_grad[: row_count - margin], own_grad[row_count - margin :] + edge_back], 0
    )
    d_proj = jnp.concatenate([d_pre, d_gate, d_decay, d_beta], 1).astype(jnp.bfloat16)
    grad_input = jnp.einsum("rd,rc->dc", hidden_one, d_proj, preferred_element_type=jnp.float32)
    one_part = jnp.einsum("rc,dc->rd", d_proj, back_input, preferred_element_type=jnp.float32)
    d_hidden_one, head_sum = (
        lax.psum(one_part.astype(jnp.bfloat16), "tp").astype(jnp.float32),
        lax.psum(d_head.astype(jnp.bfloat16), "tp").astype(jnp.float32),
    )
    grad_gain_one = jnp.sum(d_hidden_one * normed_one, 0)
    dn_one = d_hidden_one * gain_one
    tokens_grad = d_middle + rms_one * (
        dn_one - normed_one * jnp.mean(dn_one * normed_one, -1, keepdims=True)
    )
    tokens_grad = tokens_grad.reshape(tokens.shape)
    edges = [
        0,
        query_cols,
        2 * query_cols,
        conv_cols,
        conv_cols + value_cols,
        conv_cols + value_cols + head_count,
        conv_cols + value_cols + 2 * head_count,
    ]
    reduced = (
        lax.psum_scatter(grad_gain_one, ("dp", "ctx"), scatter_dimension=0, tiled=True),
        lax.psum_scatter(grad_gain_two, ("dp", "ctx"), scatter_dimension=0, tiled=True),
        lax.psum_scatter(
            grad_input[:, edges[0] : edges[1]], ("dp", "ctx"), scatter_dimension=0, tiled=True
        ),
        lax.psum_scatter(
            grad_input[:, edges[1] : edges[2]], ("dp", "ctx"), scatter_dimension=0, tiled=True
        ),
        lax.psum_scatter(
            grad_input[:, edges[2] : edges[3]], ("dp", "ctx"), scatter_dimension=0, tiled=True
        ),
        lax.psum_scatter(
            grad_input[:, edges[3] : edges[4]], ("dp", "ctx"), scatter_dimension=0, tiled=True
        ),
        lax.psum_scatter(
            grad_input[:, edges[4] : edges[5]], ("dp", "ctx"), scatter_dimension=0, tiled=True
        ),
        lax.psum_scatter(
            grad_input[:, edges[5] : edges[6]], ("dp", "ctx"), scatter_dimension=0, tiled=True
        ),
        lax.psum_scatter(grad_output, ("dp", "ctx"), scatter_dimension=0, tiled=True),
        lax.psum_scatter(grad_hgate, ("dp", "ctx"), scatter_dimension=0, tiled=True),
        lax.psum_scatter(grad_hup, ("dp", "ctx"), scatter_dimension=0, tiled=True),
        lax.psum_scatter(grad_down, ("dp", "ctx"), scatter_dimension=0, tiled=True),
    )
    conv_total, log_total, bias_total, head_total = lax.psum(
        (d_conv, d_log, d_bias, head_sum), ("dp", "ctx")
    )
    return (
        block_out,
        tokens_grad,
        reduced[0],
        reduced[1],
        reduced[2],
        reduced[3],
        reduced[4],
        reduced[5],
        reduced[6],
        reduced[7],
        reduced[8],
        conv_total[:, :query_cols],
        conv_total[:, query_cols : 2 * query_cols],
        conv_total[:, 2 * query_cols :],
        log_total,
        bias_total,
        head_total,
        reduced[9],
        reduced[10],
        reduced[11],
    )


def solution(mesh):
    return jax.shard_map(
        local,
        mesh=mesh,
        in_specs=(
            P("dp", "ctx", None),
            P("dp", None),
            P("dp", "ctx", None),
            P(("dp", "ctx")),
            P(("dp", "ctx")),
            P(("dp", "ctx"), "tp"),
            P(("dp", "ctx"), "tp"),
            P(("dp", "ctx"), "tp"),
            P(("dp", "ctx"), "tp"),
            P(("dp", "ctx"), "tp"),
            P(("dp", "ctx"), "tp"),
            P(("dp", "ctx"), "tp"),
            P(None, "tp"),
            P(None, "tp"),
            P(None, "tp"),
            P("tp"),
            P("tp"),
            P(),
            P(("dp", "ctx"), "tp"),
            P(("dp", "ctx"), "tp"),
            P(("dp", "ctx"), "tp"),
        ),
        out_specs=(
            P("dp", "ctx", None),
            P("dp", "ctx", None),
            P(("dp", "ctx")),
            P(("dp", "ctx")),
            P(("dp", "ctx"), "tp"),
            P(("dp", "ctx"), "tp"),
            P(("dp", "ctx"), "tp"),
            P(("dp", "ctx"), "tp"),
            P(("dp", "ctx"), "tp"),
            P(("dp", "ctx"), "tp"),
            P(("dp", "ctx"), "tp"),
            P(None, "tp"),
            P(None, "tp"),
            P(None, "tp"),
            P("tp"),
            P("tp"),
            P(),
            P(("dp", "ctx"), "tp"),
            P(("dp", "ctx"), "tp"),
            P(("dp", "ctx"), "tp"),
        ),
        check_vma=False,
    )
```

profile of v0, /device:TPU:0, one launch (start us, length us, event | category | flops | bytes accessed | tf_op | source)
XLA Modules:
  0.0 1123.0 jit_solution(16352454490159363568)
XLA Ops:
  9.9 10.4 all-gather
  21.5 9.7 all_gather.47
  31.2 9.2 all_gather.48
  40.4 8.5 all_gather.51
  49.1 8.1 all_gather.52
  58.5 2.9 all-gather.9.cloned.1.call-done
  61.4 6.4 concatenate.28
  67.8 3.5 fusion.282
  71.4 2.3 collective-permute-start
  76.2 2.4 fusion.228
  87.9 110.8 %while.123 = (s32[]{:T(128)}, f32[2,128,384]{2,1,0:T(8,128)S(1)}, f32[4,64,2,384]{3,1,0,2:T(8,128)}, pred[4,64,64,2]{2,1,3,0:T(32,128)(4,1)S(1)}, f32[4,64,64,2]...) while((s32[]{:T(128)}, f32[2,128,384]{2,1,0:T(8,128)S(1)}, ...), condition=%wide.region_6.7_spmd.clone.clone, body=%wide.region_3.6_spmd.clone.clone.sunk | while | flops 390947136 | bytes 9695425 | solution.py:112
  99.8 2.1 bitcast_dynamic-update-slice_fusion.53
  127.5 2.1 bitcast_dynamic-update-slice_fusion.53
  155.1 2.1 bitcast_dynamic-update-slice_fusion.53
  199.7 2.1 collective-permute-start.1
  205.0 2.1 multiply_reduce_fusion.9
  208.3 2.8 fusion.283
  213.1 9.0 all-gather.1
  222.1 41.1 %all-reduce.28.cloned.1.call-done = f32[256,1024]{1,0:T(8,128)} async-done(((f32[256,1024]{1,0:T(8,128)}), f32[256,1024]{1,0:T(8,128)}) %all-reduce.28.cloned.1.call-update) | async-done | bytes 1048592 | tf_op jit(solution)/shard_map/psum | solution.py:242
  266.4 23.0 %all-gather.15.cloned.1.call-done = bf16[1024,704]{0,1:T(8,128)(2,1)} async-done(((bf16[128,704]{0,1:T(8,128)(2,1)}), bf16[1024,704]{0,1:T(8,128)(2,1)}) %all-gather.15.cloned.1.call-update) | async-done | bytes 1441808 | tf_op jit(solution)/shard_map/all_gather | solution.py:198
  289.4 3.0 fusion.284
  292.4 24.0 %all-gather.17.cloned.1.call-done = bf16[1024,704]{0,1:T(8,128)(2,1)} async-done(((bf16[128,704]{0,1:T(8,128)(2,1)}), bf16[1024,704]{0,1:T(8,128)(2,1)}) %all-gather.17.cloned.1.call-update) | async-done | bytes 1441808 | tf_op jit(solution)/shard_map/all_gather | solution.py:199
  316.4 3.0 fusion.285
  319.4 24.1 %all-gather.19.cloned.1.call-done = bf16[1024,704]{0,1:T(8,128)(2,1)} async-done(((bf16[128,704]{0,1:T(8,128)(2,1)}), bf16[1024,704]{0,1:T(8,128)(2,1)}) %all-gather.19.cloned.1.call-update) | async-done | bytes 1441808 | tf_op jit(solution)/shard_map/all_gather | solution.py:200
  343.5 3.5 multiply_convert_fusion.1
  354.1 48.3 %all-reduce.30.cloned.1.call-done = f32[256,1024]{1,0:T(8,128)} async-done(((f32[256,1024]{1,0:T(8,128)}), f32[256,1024]{1,0:T(8,128)}) %all-reduce.30.cloned.1.call-update) | async-done | bytes 1048592 | tf_op jit(solution)/shard_map/psum | solution.py:285
  412.0 2.3 convolution_add_fusion.24
  422.5 183.6 %while.122 = (s32[]{:T(128)}, f32[2,128,384]{2,1,0:T(8,128)S(1)}, f32[4,64,2,128]{3,1,2,0:T(8,128)}, f32[4,64,2,128]{3,1,2,0:T(8,128)}, f32[4,64,2,384]{3,1,0,2:...) while((s32[]{:T(128)}, f32[2,128,384]{2,1,0:T(8,128)S(1)}, ...), condition=%wide.region_24.25_spmd, body=%wide.region_14.24_spmd.sunk | while | flops 781934592 | bytes 16670181 | solution.py:112
  630.2 2.7 copy-done
  634.0 2.8 convolution_convert_fusion.1
  637.9 4.0 convolution_convert_fusion
  641.9 3.2 fusion.278
  645.9 4.9 fusion.277
  655.0 2.1 fusion.289
  658.2 2.1 fusion.288
  661.3 2.2 convolution_bitcast_fusion.8
  665.4 10.0 psum.70
  677.0 27.6 %reduce-scatter.33.cloned.1.call-done = f32[128,2]{1,0:T(8,128)} async-done(((f32[1024,2]{1,0:T(8,128)}), f32[128,2]{1,0:T(8,128)}) %reduce-scatter.33.cloned.1.call-update) | async-done | bytes 1040
  706.1 53.5 %all-reduce.32.cloned.1.call-done = (bf16[256,1024]{1,0:T(8,128)(2,1)}, bf16[256,1024]{1,0:T(8,128)(2,1)}) async-done(((bf16[256,1024]{1,0:T(8,128)(2,1)}, bf16[256,1024]{1,0:T(8,128)(2,1)}), (bf16[256,1024]{1,0:T(8,128)(2,1)}, bf16[256,1024]{1,0:T(8,128)(2,1)})) %all-reduce.32.cloned.1.call-update) | async-done | bytes 1048592 | tf_op jit(solution)/shard_map/psum | solution.py:253
  761.2 24.2 %all-reduce.22 = (f32[1024]{0:T(1024)S(1)}, f32[1024]{0:T(1024)S(1)}, f32[4,1024]{1,0:T(4,128)S(1)}, f32[2]{0:T(128)}, f32[2]{0:T(128)}, /*index=5*/f32[256]{0:T(256)}) all-reduce(f32[1024]{0:T(1024)S(1)} %get-tuple-element.2380, f32[1024]{0:T(1024)S(1)} %get-tuple-element.2376, ...), channel_id=2, replica_groups=mesh['dp'=4,'ctx'=2,'tp'=4] {'dp','ctx'}, use_global_device_ids=true, to_apply=%region_30.31.clone | all-reduce | flops 6404 | bytes 50720
  791.0 6.8 reduce-scatter.15.cloned.1.call-done
  799.5 37.5 %reduce-scatter.17.cloned.1.call-done = f32[128,256]{0,1:T(8,128)} async-done(((f32[1024,256]{0,1:T(8,128)}), f32[128,256]{0,1:T(8,128)}) %reduce-scatter.17.cloned.1.call-update) | async-done | bytes 131088 | tf_op jit(solution)/shard_map/reduce_scatter | solution.py:338
  838.7 42.6 %reduce-scatter.19.cloned.1.call-done = f32[128,512]{0,1:T(8,128)} async-done(((f32[1024,512]{0,1:T(8,128)}), f32[128,512]{0,1:T(8,128)}) %reduce-scatter.19.cloned.1.call-update) | async-done | bytes 262160 | tf_op jit(solution)/shard_map/reduce_scatter | solution.py:341
  883.1 42.5 %reduce-scatter.21.cloned.1.call-done = f32[128,512]{0,1:T(8,128)} async-done(((f32[1024,512]{0,1:T(8,128)}), f32[128,512]{0,1:T(8,128)}) %reduce-scatter.21.cloned.1.call-update) | async-done | bytes 262160 | tf_op jit(solution)/shard_map/reduce_scatter | solution.py:344
  927.4 43.1 %reduce-scatter.23.cloned.1.call-done = f32[128,512]{1,0:T(8,128)} async-done(((f32[1024,512]{1,0:T(8,128)}), f32[128,512]{1,0:T(8,128)}) %reduce-scatter.23.cloned.1.call-update) | async-done | bytes 262160 | tf_op jit(solution)/shard_map/reduce_scatter | solution.py:353
  970.5 48.5 %reduce-scatter.27.cloned.1.call-done = f32[128,704]{0,1:T(8,128)} async-done(((f32[1024,704]{0,1:T(8,128)}), f32[128,704]{0,1:T(8,128)}) %reduce-scatter.27.cloned.1.call-update) | async-done | bytes 360464 | tf_op jit(solution)/shard_map/reduce_scatter | solution.py:355
  1019.0 48.6 %reduce-scatter.25.cloned.1.call-done = f32[128,704]{0,1:T(8,128)} async-done(((f32[1024,704]{0,1:T(8,128)}), f32[128,704]{0,1:T(8,128)}) %reduce-scatter.25.cloned.1.call-update) | async-done | bytes 360464 | tf_op jit(solution)/shard_map/reduce_scatter | solution.py:354
  1067.6 48.7 %reduce-scatter.29.cloned.1.call-done = f32[128,704]{0,1:T(8,128)} async-done(((f32[1024,704]{0,1:T(8,128)}), f32[128,704]{0,1:T(8,128)}) %reduce-scatter.29.cloned.1.call-update) | async-done | bytes 360464 | tf_op jit(solution)/shard_map/reduce_scatter | solution.py:356
  (819 shorter events, 389.2 us)
Async XLA Ops:
  7.2 24.1 %copy-start.45 = (bf16[128,256]{1,0:T(8,128)(2,1)S(1)}, bf16[128,256]{1,0:T(8,128)(2,1)}, u32[]{:S(2)}) copy-start(bf16[128,256]{1,0:T(8,128)(2,1)} %param.31) | copy-start | bytes 196612
  7.2 33.2 %copy-start.81 = (bf16[128,2]{0,1:T(2,128)(2,1)S(1)}, bf16[128,2]{0,1:T(2,128)(2,1)}, u32[]{:S(2)}) copy-start(bf16[128,2]{0,1:T(2,128)(2,1)} %param.34) | copy-start | bytes 1540
  7.2 41.9 %copy-start.82 = (bf16[128,2]{0,1:T(2,128)(2,1)S(1)}, bf16[128,2]{0,1:T(2,128)(2,1)}, u32[]{:S(2)}) copy-start(bf16[128,2]{0,1:T(2,128)(2,1)} %param.35) | copy-start | bytes 1540
  7.2 50.2 %copy-start.80 = (s32[1,512]{1,0:T(1,128)S(1)}, s32[1,512]{1,0:T(1,128)}, u32[]{:S(2)}) copy-start(s32[1,512]{1,0:T(1,128)} %param.26) | copy-start | bytes 6148
  7.2 50.4 %copy-start.74 = (f32[4,256]{1,0:T(4,128)S(1)}, f32[4,256]{1,0:T(4,128)}, u32[]{:S(2)}) copy-start(f32[4,256]{1,0:T(4,128)} %param.37) | copy-start | bytes 12292
  7.2 50.4 %copy-start.75 = (f32[4,256]{1,0:T(4,128)S(1)}, f32[4,256]{1,0:T(4,128)}, u32[]{:S(2)}) copy-start(f32[4,256]{1,0:T(4,128)} %param.38) | copy-start | bytes 12292
  7.3 50.4 %copy-start.72 = (f32[4,512]{1,0:T(4,128)S(1)}, f32[4,512]{1,0:T(4,128)}, u32[]{:S(2)}) copy-start(f32[4,512]{1,0:T(4,128)} %param.39) | copy-start | bytes 24580
  7.3 50.4 %copy-start.85 = (f32[2]{0:T(128)S(1)}, f32[2]{0:T(128)}, u32[]{:S(2)}) copy-start(f32[2]{0:T(128)} %param.40) | copy-start | bytes 28
  7.3 51.2 %all-gather.11.cloned.1.call-start = ((), (), s32[]{:S(2)}) async-start(), calls=%async_computation.11 | async-start | bytes 1179648 | tf_op jit(solution)/shard_map/all_gather | solution.py:194
  8.0 53.4 %all-gather.9.cloned.1.call-start = ((), (), s32[]{:S(2)}) async-start(), calls=%async_computation.10 | async-start | bytes 1179648 | tf_op jit(solution)/shard_map/all_gather | solution.py:193
  8.8 199.5 %all-gather.13.cloned.1.call-start = ((), (), s32[]{:S(2)}) async-start(), calls=%async_computation.12 | async-start | bytes 1179648 | tf_op jit(solution)/shard_map/all_gather | solution.py:197
  9.5 253.7 %all-reduce.28.cloned.1.call-start = ((), (), s32[]{:S(2)}) async-start(), calls=%async_computation.13 | async-start | bytes 2097152 | tf_op jit(solution)/shard_map/psum | solution.py:242
  57.6 18.6 %copy-start.64 = (f32[256]{0:T(256)}, f32[256]{0:T(256)S(1)}, u32[]{:S(2)}) copy-start(f32[256]{0:T(256)S(1)} %get-tuple-element.2670) | copy-start | bytes 3076
  57.6 18.6 %copy-start.66 = (f32[256]{0:T(256)}, f32[256]{0:T(256)S(1)}, u32[]{:S(2)}) copy-start(f32[256]{0:T(256)S(1)} %get-tuple-element.2671) | copy-start | bytes 3076
  57.6 18.6 %copy-start.68 = (f32[256]{0:T(256)}, f32[256]{0:T(256)S(1)}, u32[]{:S(2)}) copy-start(f32[256]{0:T(256)S(1)} %get-tuple-element.2672) | copy-start | bytes 3076
  57.7 18.5 %copy-start.46 = (f32[1,1024]{1,0:T(1,128)}, f32[1,1024]{1,0:T(1,128)S(1)}, u32[]{:S(2)}) copy-start(f32[1,1024]{1,0:T(1,128)S(1)} %get-tuple-element.2664) | copy-start | bytes 12292
  57.7 18.5 %copy-start.48 = (f32[1,1024]{1,0:T(1,128)}, f32[1,1024]{1,0:T(1,128)S(1)}, u32[]{:S(2)}) copy-start(f32[1,1024]{1,0:T(1,128)S(1)} %get-tuple-element.2665) | copy-start | bytes 12292
  57.7 18.5 %copy-start.50 = (f32[1,1024]{1,0:T(1,128)}, f32[1,1024]{1,0:T(1,128)S(1)}, u32[]{:S(2)}) copy-start(f32[1,1024]{1,0:T(1,128)S(1)} %get-tuple-element.2666) | copy-start | bytes 12292
  57.7 16.0 %copy-start.78 = (f32[2]{0:T(128)}, f32[2]{0:T(128)S(1)}, u32[]{:S(2)}) copy-start(f32[2]{0:T(128)S(1)} %exponential_negate_fusion) | copy-start | bytes 28
  71.4 4.4 collective-permute-start
  199.7 5.3 collective-permute-start.1
  211.1 78.3 %all-gather.15.cloned.1.call-start = ((), (), s32[]{:S(2)}) async-start(), calls=%async_computation.14 | async-start | bytes 1622016 | tf_op jit(solution)/shard_map/all_gather | solution.py:198
  211.7 104.7 %all-gather.17.cloned.1.call-start = ((), (), s32[]{:S(2)}) async-start(), calls=%async_computation.15 | async-start | bytes 1622016 | tf_op jit(solution)/shard_map/all_gather | solution.py:199
  212.3 131.2 %all-gather.19.cloned.1.call-start = ((), (), s32[]{:S(2)}) async-start(), calls=%async_computation.16 | async-start | bytes 1622016 | tf_op jit(solution)/shard_map/all_gather | solution.py:200
  213.0 189.3 %all-reduce.30.cloned.1.call-start = ((), (), s32[]{:S(2)}) async-start(), calls=%async_computation.17 | async-start | bytes 2097152 | tf_op jit(solution)/shard_map/psum | solution.py:285
  264.8 139.3 %copy-start.1 = (f32[256,1024]{1,0:T(8,128)}, f32[256,1024]{1,0:T(8,128)S(1)}, u32[]{:S(2)}) copy-start(f32[256,1024]{1,0:T(8,128)S(1)} %get-tuple-element.2582) | copy-start | bytes 3145732
  350.3 325.2 %reduce-scatter.31.cloned.1.call-start = ((), (), s32[]{:S(2)}) async-start(), calls=%async_computation.26 | async-start | bytes 589824
  414.3 3.7 collective-permute-start.2
  428.4 10.5 copy-start.21
  429.6 11.2 copy-start.32
  474.3 10.5 copy-start.21
  475.5 11.2 copy-start.32
  521.3 11.2 copy-start.32
  567.1 11.2 copy-start.32
  624.2 3.8 collective-permute-start.3
  633.9 70.7 %reduce-scatter.33.cloned.1.call-start = ((), (), s32[]{:S(2)}) async-start(), calls=%async_computation.27 | async-start | bytes 589824
  637.8 121.8 %all-reduce.32.cloned.1.call-start = ((), (), s32[]{:S(2)}) async-start(), calls=%async_computation.28 | async-start | bytes 2097152 | tf_op jit(solution)/shard_map/psum | solution.py:253
  641.9 156.0 %reduce-scatter.15.cloned.1.call-start = ((), (), s32[]{:S(2)}) async-start(), calls=%async_computation.18 | async-start | bytes 1179648 | tf_op jit(solution)/shard_map/reduce_scatter | solution.py:335
  645.1 191.9 %reduce-scatter.17.cloned.1.call-start = ((), (), s32[]{:S(2)}) async-start(), calls=%async_computation.19 | async-start | bytes 1179648 | tf_op jit(solution)/shard_map/reduce_scatter | solution.py:338
  645.9 235.5 %reduce-scatter.19.cloned.1.call-start = ((), (), s32[]{:S(2)}) async-start(), calls=%async_computation.20 | async-start | bytes 2359296 | tf_op jit(solution)/shard_map/reduce_scatter | solution.py:341
  650.9 274.8 %reduce-scatter.21.cloned.1.call-start = ((), (), s32[]{:S(2)}) async-start(), calls=%async_computation.21 | async-start | bytes 2359296 | tf_op jit(solution)/shard_map/reduce_scatter | solution.py:344
  651.4 319.0 %reduce-scatter.23.cloned.1.call-start = ((), (), s32[]{:S(2)}) async-start(), calls=%async_computation.22 | async-start | bytes 2359296 | tf_op jit(solution)/shard_map/reduce_scatter | solution.py:353
  653.9 365.1 %reduce-scatter.27.cloned.1.call-start = ((), (), s32[]{:S(2)}) async-start(), calls=%async_computation.24 | async-start | bytes 3244032 | tf_op jit(solution)/shard_map/reduce_scatter | solution.py:355
  657.2 410.4 %reduce-scatter.25.cloned.1.call-start = ((), (), s32[]{:S(2)}) async-start(), calls=%async_computation.23 | async-start | bytes 3244032 | tf_op jit(solution)/shard_map/reduce_scatter | solution.py:354
  660.3 456.0 %reduce-scatter.29.cloned.1.call-start = ((), (), s32[]{:S(2)}) async-start(), calls=%async_computation.25 | async-start | bytes 3244032 | tf_op jit(solution)/shard_map/reduce_scatter | solution.py:356
  663.5 12.0 %copy-start.86 = (f32[2]{0:T(128)S(1)}, f32[2]{0:T(128)}, u32[]{:S(2)}) copy-start(f32[2]{0:T(128)} %param.40) | copy-start | bytes 28
  663.5 124.3 %copy-start.2 = (f32[256,1024]{1,0:T(8,128)S(1)}, f32[256,1024]{1,0:T(8,128)}, u32[]{:S(2)}) copy-start(f32[256,1024]{1,0:T(8,128)} %copy-done.1) | copy-start | bytes 3145732
  759.6 30.2 %copy-start.31 = (bf16[256,1024]{1,0:T(8,128)(2,1)S(1)}, bf16[256,1024]{1,0:T(8,128)(2,1)}, u32[]{:S(2)}) copy-start(bf16[256,1024]{1,0:T(8,128)(2,1)} %get-tuple-element.2573) | copy-start | bytes 1572868
  (75 other events, 269.3 us)
Sparse Core Ops, SparseCore 0:
  10.0 26.0 all-gather.10
  38.0 23.3 all-gather.8
  63.3 23.3 all-gather.12
  211.2 51.9 all-reduce.27
  264.9 24.4 all-gather.14
  291.2 25.1 all-gather.16
  318.3 25.1 all-gather.18
  350.4 51.8 all-reduce.29
  634.1 33.4 reduce-scatter.30
  670.4 34.1 reduce-scatter.32
  707.6 51.9 all-reduce.31
  762.6 35.1 reduce-scatter.14
  801.0 35.9 reduce-scatter.16
  840.2 41.1 reduce-scatter.18
  884.5 41.1 reduce-scatter.20
  929.3 41.0 reduce-scatter.22
  974.3 44.6 reduce-scatter.26
  1022.8 44.6 reduce-scatter.24
  1071.5 44.6 reduce-scatter.28
where the time goes:
time: 1130 us; the launch traced here: 1120 us
  waiting for transfers between devices  569 us (50%)
  matrix products  249 us (22%)
  local copies, waits for them, and re-layouts  128 us (11%)
  blocking collectives  89.1 us (8%)
  other arithmetic  61.4 us (5%)
  between operations  16.4 us (1%)
    dot_general x60, matrix products, unit_lower_inverse(): jnp.einsum('hij,hjk->hik', inverse, power, precision=HIGHEST)  57.8 us
    psum x1, waiting for transfers between devices, local(): feed = lax.psum(feed_part.astype(jnp.bfloat16), 'tp').astype(jnp.float32)  53.5 us
    reduce_scatter x1, waiting for transfers between devices, local(): lax.psum_scatter(grad_down, ('dp', 'ctx'), scatter_dimension=0, tiled=True)  48.7 us
    reduce_scatter x1, waiting for transfers between devices, local(): lax.psum_scatter(grad_hgate, ('dp', 'ctx'), scatter_dimension=0, tiled=True)  48.6 us
    reduce_scatter x1, waiting for transfers between devices, local(): lax.psum_scatter(grad_hup, ('dp', 'ctx'), scatter_dimension=0, tiled=True)  48.5 us
    psum x1, waiting for transfers between devices, local(): d_hidden_two = lax.psum(two_part, 'tp')  48.3 us
    reduce_scatter x1, waiting for transfers between devices, local(): lax.psum_scatter(grad_output, ('dp', 'ctx'), scatter_dimension=0, tiled=T...  43.1 us
    reduce_scatter x1, waiting for transfers between devices, local(): lax.psum_scatter(grad_input[:, edges[2]:edges[3]], ('dp', 'ctx'), scatter...  42.6 us
  transfers between devices with their start and end apart: 23, of which 17 were waited for; matrix products, arithmetic and copies ran while one was open for 18% of the time, Pallas kernels for 0%

commit v1 on v0

v1 whole, which is shorter than its diff:
```python
from functools import partial

import jax
import jax.numpy as jnp
from jax import lax
from jax.sharding import PartitionSpec as P

GROUP = 64


EPSILON = 1e-06
HIGHEST = lax.Precision.HIGHEST
HIGH = lax.Precision.HIGH
LANES = 128


def passed_along(value, axis, by):
    devices = lax.axis_size(axis)
    pairs = [(i, i + by) for i in range(devices) if 0 <= i + by < devices]
    return lax.ppermute(value, axis, pairs)


def features(pre_ext, seg_ext, conv_weight, decay_lin, beta_lin, decay_log, decay_bias, key_dim):
    margin = conv_weight.shape[0] - 1
    row_count = pre_ext.shape[0] - margin
    head_count = decay_lin.shape[1]
    own_segment = seg_ext[margin:]
    convolved = jnp.zeros((row_count, pre_ext.shape[1]), jnp.float32)
    for lag in range(margin + 1):
        first_row = margin - lag
        same_doc = (seg_ext[first_row : first_row + row_count] == own_segment).astype(jnp.float32)
        convolved = (
            convolved
            + conv_weight[lag][None, :]
            * pre_ext[first_row : first_row + row_count]
            * same_doc[:, None]
        )
    activated = jax.nn.silu(convolved)
    query_cols = head_count * key_dim
    queries = activated[:, :query_cols].reshape(row_count, head_count, key_dim)
    key_rows = activated[:, query_cols : 2 * query_cols].reshape(row_count, head_count, key_dim)
    value_rows = activated[:, 2 * query_cols :].reshape(row_count, head_count, -1)
    queries = (
        queries
        * lax.rsqrt(jnp.sum(queries * queries, -1, keepdims=True) + EPSILON)
        * key_dim ** (-0.5)
    )
    key_rows = key_rows * lax.rsqrt(jnp.sum(key_rows * key_rows, -1, keepdims=True) + EPSILON)
    decay_rate = -jnp.exp(decay_log)[None, :] * jax.nn.softplus(decay_lin + decay_bias[None, :])
    beta_gate = jax.nn.sigmoid(beta_lin)
    starts = (own_segment != seg_ext[margin - 1 : margin - 1 + row_count]).astype(jnp.float32)
    return (queries, key_rows, value_rows, decay_rate, beta_gate, starts)


def lower_inverse_value(lower_part):
    order = lower_part.shape[-1]
    negated = -lower_part
    inverse = jnp.eye(order, dtype=jnp.float32)[None] + negated
    power = negated
    span = 2
    while span < order:
        power = jnp.einsum("bij,bjk->bik", power, power, precision=HIGHEST)
        inverse = inverse + jnp.einsum("bij,bjk->bik", inverse, power, precision=HIGHEST)
        span = span * 2
    return inverse


@jax.custom_vjp
def unit_lower_inverse(lower_part):
    return lower_inverse_value(lower_part)


def inverse_forward(lower_part):
    inverse = lower_inverse_value(lower_part)
    return inverse, inverse


def inverse_backward(inverse, grad):
    half = jnp.einsum("bji,bjk->bik", inverse, grad, precision=HIGHEST)
    return (-jnp.einsum("bij,bkj->bik", half, inverse, precision=HIGHEST),)


unit_lower_inverse.defvjp(inverse_forward, inverse_backward)


def mm(spec, left, right):
    return jnp.einsum(spec, left, right, precision=HIGH)


def group_maps(queries, key_rows, value_rows, decay_rate, beta_gate, starts, group):
    row_count, head_count, key_dim = queries.shape
    blocks = row_count // group

    def batched(member):
        tail = member.shape[2:]
        split = member.reshape((blocks, group, head_count) + tail)
        moved = jnp.moveaxis(split, 2, 1)
        return moved.reshape((blocks * head_count, group) + tail)

    queries, key_rows, value_rows = batched(queries), batched(key_rows), batched(value_rows)
    position = jnp.arange(group)
    until = (position[None, :] <= position[:, None]).astype(jnp.float32)
    beta = batched(beta_gate)
    cumulative = jnp.einsum("ts,bs->bt", until, batched(decay_rate), precision=HIGHEST)
    counted = jnp.cumsum(starts.reshape(blocks, group), axis=1)
    counted = jnp.broadcast_to(counted[:, None, :], (blocks, head_count, group))
    counted = counted.reshape(blocks * head_count, group)
    same_doc = (counted[:, :, None] == counted[:, None, :]) & (
        position[None, None, :] <= position[None, :, None]
    )
    same_value = same_doc.astype(jnp.float32)
    strictly = same_value * (position[None, :] < position[:, None]).astype(jnp.float32)[None]
    spread = cumulative[:, :, None] - cumulative[:, None, :]
    decay_pair = jnp.exp(jnp.where(same_doc, spread, 0.0)) * same_value
    anchor = jnp.exp(cumulative) * (counted == 0).astype(jnp.float32)
    closing = decay_pair[:, group - 1, :]
    key_gram = mm("btd,bjd->btj", key_rows, key_rows)
    inverse = unit_lower_inverse(beta[:, :, None] * decay_pair * key_gram * strictly)
    right = beta[:, :, None] * jnp.concatenate([-anchor[:, :, None] * key_rows, value_rows], 2)
    updates = mm("btj,bjw->btw", inverse, right)
    query_key = mm("btd,bjd->btj", queries, key_rows) * decay_pair
    from_rows = mm("btj,bjw->btw", query_key, updates)
    carried = from_rows[:, :, :key_dim] + anchor[:, :, None] * queries
    local_out = from_rows[:, :, key_dim:]
    maps = mm("bjd,bjw->bdw", key_rows * closing[:, :, None], updates)
    last = anchor[:, group - 1]
    transfer = maps[:, :, :key_dim] + last[:, None, None] * jnp.eye(key_dim, dtype=jnp.float32)
    offset = maps[:, :, key_dim:]

    def grouped(member):
        return member.reshape((blocks, head_count) + member.shape[1:])

    return grouped(carried), grouped(local_out), grouped(transfer), grouped(offset)


def compose(carried, local_out, transfer, offset):
    blocks = carried.shape[0]
    key_dim = carried.shape[-1]
    running = jnp.concatenate([transfer[0], offset[0]], 2)
    before = []
    for block in range(1, blocks):
        before.append(running)
        running = mm("hde,hew->hdw", transfer[block], running)
        running = jnp.concatenate(
            [running[:, :, :key_dim], running[:, :, key_dim:] + offset[block]], 2
        )
    if blocks > 1:
        mixed_in = mm("ghtd,ghdw->ghtw", carried[1:], jnp.stack(before))
        carried = jnp.concatenate([carried[:1], mixed_in[..., :key_dim]], 0)
        local_out = jnp.concatenate(
            [local_out[:1], local_out[1:] + mixed_in[..., key_dim:]], 0
        )
    return carried, local_out, running[:, :, :key_dim], running[:, :, key_dim:]


def gated(output_rows, gate_lin, head_gain):
    row_count, head_count, value_dim = output_rows.shape
    scaled = output_rows * lax.rsqrt(
        jnp.mean(output_rows * output_rows, -1, keepdims=True) + EPSILON
    )
    gate_rows = gate_lin.reshape(row_count, head_count, value_dim)
    return (scaled * head_gain * jax.nn.silu(gate_rows)).reshape(row_count, head_count * value_dim)


def expand(
    pre_ext, decay_lin, beta_lin, conv_weight, decay_log, decay_bias, seg_ext, key_dim, group
):
    queries, key_rows, value_rows, decay_rate, beta_gate, starts = features(
        pre_ext, seg_ext, conv_weight, decay_lin, beta_lin, decay_log, decay_bias, key_dim
    )
    return compose(
        *group_maps(queries, key_rows, value_rows, decay_rate, beta_gate, starts, group)
    )


def finish(carried, local_out, initial, gate_lin, head_gain):
    output_rows = local_out + mm("ghtd,hdw->ghtw", carried, initial)
    blocks, head_count, group, value_dim = output_rows.shape
    output_rows = jnp.transpose(output_rows, (0, 2, 1, 3)).reshape(
        blocks * group, head_count, value_dim
    )
    return gated(output_rows, gate_lin, head_gain)


def apply_map(matrix, addend, incoming):
    return mm("hde,hew->hdw", matrix, incoming) + addend


def local(
    tokens,
    segments,
    cotangent,
    mixer_gain,
    mlp_gain,
    query_weight,
    key_weight,
    value_weight,
    gate_weight,
    decay_weight,
    beta_weight,
    output_weight,
    conv_query,
    conv_key,
    conv_value,
    decay_log,
    decay_bias,
    head_gain,
    hidden_gate,
    hidden_up,
    hidden_down,
):
    width = tokens.shape[-1]
    inputs = tokens.reshape(-1, width).astype(jnp.float32)
    row_count = inputs.shape[0]
    query_cols = query_weight.shape[1]
    value_cols = value_weight.shape[1]
    head_count = decay_weight.shape[1]
    ff_cols = hidden_gate.shape[1]
    axes = ("dp", "ctx")
    used = 2 * query_cols + 2 * value_cols + 2 * head_count + 2
    pad_cols = -used % LANES
    own_rows = query_weight.shape[0]
    in_weights = lax.all_gather(
        jnp.concatenate(
            [
                query_weight,
                key_weight,
                value_weight,
                gate_weight,
                decay_weight,
                beta_weight,
                mixer_gain[:, None],
                mlp_gain[:, None],
                jnp.zeros((own_rows, pad_cols), jnp.bfloat16),
            ],
            1,
        ),
        axes,
        axis=0,
        tiled=True,
    )
    full_output = lax.all_gather(output_weight, axes, axis=0, tiled=True)
    full_gate_up = lax.all_gather(
        jnp.concatenate([hidden_gate, hidden_up], 1), axes, axis=0, tiled=True
    )
    full_hidden_down = lax.all_gather(hidden_down, axes, axis=0, tiled=True)
    gain_one = in_weights[:, used - 2].astype(jnp.float32)
    gain_two = in_weights[:, used - 1].astype(jnp.float32)
    conv_cols = 2 * query_cols + value_cols
    key_dim = query_cols // head_count
    rms_one = lax.rsqrt(jnp.mean(inputs * inputs, -1, keepdims=True) + EPSILON)
    normed_one = inputs * rms_one
    hidden_one = (normed_one * gain_one).astype(jnp.bfloat16)
    projected = jnp.dot(hidden_one, in_weights, preferred_element_type=jnp.float32)
    pre_conv = projected[:, :conv_cols].astype(jnp.bfloat16)
    gate_lin = projected[:, conv_cols : conv_cols + value_cols]
    decay_lin = projected[:, conv_cols + value_cols : conv_cols + value_cols + head_count]
    beta_lin = projected[:, used - 2 - head_count : used - 2]
    conv_weight = jnp.concatenate([conv_query, conv_key, conv_value], 1)
    margin = conv_weight.shape[0] - 1
    edge_rows = passed_along(pre_conv[row_count - margin :], "ctx", 1)
    pre_ext = jnp.concatenate([edge_rows, pre_conv], 0).astype(jnp.float32)
    seg_padded = jnp.concatenate([jnp.full((margin,), -1, jnp.int32), segments.reshape(-1)], 0)
    seg_ext = lax.dynamic_slice_in_dim(
        seg_padded, lax.axis_index("ctx") * row_count, row_count + margin
    )
    expand_fn = partial(expand, seg_ext=seg_ext, key_dim=key_dim, group=GROUP)
    (carried, local_out, transfer, offset), expand_back = jax.vjp(
        expand_fn, pre_ext, decay_lin, beta_lin, conv_weight, decay_log, decay_bias
    )

    initial = jnp.zeros_like(offset)
    for _ in range(lax.axis_size("ctx") - 1):
        initial = passed_along(apply_map(transfer, offset, initial), "ctx", 1)
    mixed, finish_back = jax.vjp(finish, carried, local_out, initial, gate_lin, head_gain)
    mixed_b = mixed.astype(jnp.bfloat16)
    mixer_part = jnp.einsum("rc,dc->rd", mixed_b, full_output, preferred_element_type=jnp.float32)
    attention = lax.psum(mixer_part.astype(jnp.bfloat16), "tp").astype(jnp.float32)
    middle = inputs + attention
    rms_two = lax.rsqrt(jnp.mean(middle * middle, -1, keepdims=True) + EPSILON)
    normed_two = middle * rms_two
    hidden_two = (normed_two * gain_two).astype(jnp.bfloat16)
    gate_up = jnp.dot(hidden_two, full_gate_up, preferred_element_type=jnp.float32)
    gate_pre = gate_up[:, :ff_cols]
    up_pre = gate_up[:, ff_cols:]
    sigma = jax.nn.sigmoid(gate_pre)
    swish = gate_pre * sigma
    activ = (swish * up_pre).astype(jnp.bfloat16)
    feed_part = jnp.einsum("rf,df->rd", activ, full_hidden_down, preferred_element_type=jnp.float32)
    grad_rows = cotangent.reshape(-1, width)
    grad_out = grad_rows.astype(jnp.float32)
    d_activ = jnp.dot(grad_rows, full_hidden_down, preferred_element_type=jnp.float32)
    d_gate_pre = (d_activ * up_pre * sigma * (1.0 + gate_pre * (1.0 - sigma))).astype(jnp.bfloat16)
    d_up_pre = (d_activ * swish).astype(jnp.bfloat16)
    grad_down = jnp.einsum("rd,rf->df", grad_rows, activ, preferred_element_type=jnp.float32)
    d_gate_up = jnp.concatenate([d_gate_pre, d_up_pre], 1)
    grad_gate_up = jnp.einsum(
        "rd,rf->df", hidden_two, d_gate_up, preferred_element_type=jnp.float32
    )
    two_part = jnp.einsum("rf,df->rd", d_gate_up, full_gate_up, preferred_element_type=jnp.float32)
    d_hidden_two = lax.psum(two_part.astype(jnp.bfloat16), "tp").astype(jnp.float32)
    grad_gain_two = jnp.sum(d_hidden_two * normed_two, 0)
    dn_two = d_hidden_two * gain_two
    d_middle = grad_out + rms_two * (
        dn_two - normed_two * jnp.mean(dn_two * normed_two, -1, keepdims=True)
    )
    d_middle_b = d_middle.astype(jnp.bfloat16)
    d_mixed = jnp.dot(d_middle_b, full_output, preferred_element_type=jnp.float32)
    grad_output = jnp.einsum("rd,rc->dc", d_middle_b, mixed_b, preferred_element_type=jnp.float32)
    d_carried, d_local, init_grad, d_gate, d_head = finish_back(d_mixed)
    transposed = jnp.transpose(transfer, (0, 2, 1))

    end_grad = jnp.zeros_like(offset)
    for _ in range(lax.axis_size("ctx") - 1):
        end_grad = passed_along(apply_map(transposed, init_grad, end_grad), "ctx", -1)
    d_transfer = mm("hdw,hew->hde", end_grad, initial)
    d_pre_ext, d_decay, d_beta, d_conv, d_log, d_bias = expand_back(
        (d_carried, d_local, d_transfer, end_grad)
    )
    edge_back = passed_along(d_pre_ext[:margin], "ctx", -1)
    own_grad = d_pre_ext[margin:]
    d_pre = jnp.concatenate(
        [own_grad[: row_count - margin], own_grad[row_count - margin :] + edge_back], 0
    )
    d_proj = jnp.concatenate(
        [d_pre, d_gate, d_decay, d_beta, jnp.zeros((row_count, 2 + pad_cols), jnp.float32)], 1
    ).astype(jnp.bfloat16)
    grad_input = jnp.einsum("rd,rc->dc", hidden_one, d_proj, preferred_element_type=jnp.float32)
    one_part = jnp.einsum("rc,dc->rd", d_proj, in_weights, preferred_element_type=jnp.float32)
    value_dim = d_head.shape[0]
    head_row = jnp.zeros((16, width), jnp.bfloat16)
    head_row = head_row.at[0, :value_dim].set(d_head.astype(jnp.bfloat16))
    one_sum = lax.psum(jnp.concatenate([one_part.astype(jnp.bfloat16), head_row], 0), "tp")
    one_sum = one_sum.astype(jnp.float32)
    d_hidden_one, head_sum = one_sum[:row_count], one_sum[row_count, :value_dim]
    feed = lax.psum(feed_part.astype(jnp.bfloat16), "tp").astype(jnp.float32)
    block_out = (middle + feed).astype(jnp.bfloat16).reshape(tokens.shape)
    grad_gain_one = jnp.sum(d_hidden_one * normed_one, 0)
    dn_one = d_hidden_one * gain_one
    tokens_grad = d_middle + rms_one * (
        dn_one - normed_one * jnp.mean(dn_one * normed_one, -1, keepdims=True)
    )
    tokens_grad = tokens_grad.reshape(tokens.shape)
    edges = [
        0,
        query_cols,
        2 * query_cols,
        conv_cols,
        conv_cols + value_cols,
        conv_cols + value_cols + head_count,
        conv_cols + value_cols + 2 * head_count,
    ]

    def scattered(member):
        total = lax.psum_scatter(
            member.astype(jnp.bfloat16), axes, scatter_dimension=0, tiled=True
        )
        return total.astype(jnp.float32)

    column = jnp.arange(grad_input.shape[1])[None, :]
    grad_input = jnp.where(column == used - 2, grad_gain_one[:, None], grad_input)
    grad_input = jnp.where(column == used - 1, grad_gain_two[:, None], grad_input)
    down_own = scattered(grad_down)
    gate_up_own = scattered(grad_gate_up)
    output_own = scattered(grad_output)
    input_own = scattered(grad_input)
    reduced = (
        input_own[:, used - 2],
        input_own[:, used - 1],
        *(input_own[:, edges[i] : edges[i + 1]] for i in range(6)),
        output_own,
        gate_up_own[:, :ff_cols],
        gate_up_own[:, ff_cols:],
        down_own,
    )
    conv_total, log_total, bias_total, head_total = lax.psum(
        (d_conv, d_log, d_bias, head_sum), ("dp", "ctx")
    )
    return (
        block_out,
        tokens_grad,
        reduced[0],
        reduced[1],
        reduced[2],
        reduced[3],
        reduced[4],
        reduced[5],
        reduced[6],
        reduced[7],
        reduced[8],
        conv_total[:, :query_cols],
        conv_total[:, query_cols : 2 * query_cols],
        conv_total[:, 2 * query_cols :],
        log_total,
        bias_total,
        head_total,
        reduced[9],
        reduced[10],
        reduced[11],
    )


def solution(mesh):
    return jax.shard_map(
        local,
        mesh=mesh,
        in_specs=(
            P("dp", "ctx", None),
            P("dp", None),
            P("dp", "ctx", None),
            P(("dp", "ctx")),
            P(("dp", "ctx")),
            P(("dp", "ctx"), "tp"),
            P(("dp", "ctx"), "tp"),
            P(("dp", "ctx"), "tp"),
            P(("dp", "ctx"), "tp"),
            P(("dp", "ctx"), "tp"),
            P(("dp", "ctx"), "tp"),
            P(("dp", "ctx"), "tp"),
            P(None, "tp"),
            P(None, "tp"),
            P(None, "tp"),
            P("tp"),
            P("tp"),
            P(),
            P(("dp", "ctx"), "tp"),
            P(("dp", "ctx"), "tp"),
            P(("dp", "ctx"), "tp"),
        ),
        out_specs=(
            P("dp", "ctx", None),
            P("dp", "ctx", None),
            P(("dp", "ctx")),
            P(("dp", "ctx")),
            P(("dp", "ctx"), "tp"),
            P(("dp", "ctx"), "tp"),
            P(("dp", "ctx"), "tp"),
            P(("dp", "ctx"), "tp"),
            P(("dp", "ctx"), "tp"),
            P(("dp", "ctx"), "tp"),
            P(("dp", "ctx"), "tp"),
            P(None, "tp"),
            P(None, "tp"),
            P(None, "tp"),
            P("tp"),
            P("tp"),
            P(),
            P(("dp", "ctx"), "tp"),
            P(("dp", "ctx"), "tp"),
            P(("dp", "ctx"), "tp"),
        ),
        check_vma=False,
    )
```

time: 1130 us -> 556 us (0.49)
  waiting for transfers between devices: 569 us -> 344 us
  matrix products: 249 us -> 65.1 us
  local copies, waits for them, and re-layouts: 128 us -> 55.3 us
  blocking collectives: 89.1 us -> 24.8 us
  other arithmetic: 61.4 us -> 39 us
    reduce_scatter x8 -> x3, waiting for transfers between devices: 318 us -> 97.4 us  [scattered(): lax.psum_scatter(member.astype(jnp.bfloat16), axes, scatter_dimension=0,...]
    dot_general x219 -> x53, matrix products: 235 us -> 49.9 us  [the longest x33 25.1 us: mm(): return jnp.einsum(spec, left, right, precision=HIGH)]
    all_gather x6 -> x0, blocking collectives: 54.9 us -> none  [the longest x1 10.4 us: local(): lax.all_gather(mixer_gain, ('dp', 'ctx'), axis=0, tiled=True)]
    unnamed x1 -> x0, blocking collectives: 24.2 us -> none
    dynamic_update_slice x44 -> x0, local copies, waits for them, and re-layouts: 22.5 us -> none  [delta_run(): last_memory, outputs = lax.scan(group_update, memory, pieces)]
    psum x2, waiting for transfers between devices: 89.4 us -> 73.2 us  [the longest x1 37.4 us: local(): lax.psum(mixer_part.astype(jnp.bfloat16), 'tp').astype(jnp.float32)]
    mul x36 -> x4, local copies, waits for them, and re-layouts: 19.9 us -> 3.84 us  [the longest x1 1.46 us: features(): lax.rsqrt(jnp.sum(queries * queries, -1, keepdims=True) + EPSILON)]
    psum x1, blocking collectives: 10 us -> 24.8 us  [local(): lax.psum((d_conv, d_log, d_bias, head_sum), ('dp', 'ctx'))]
  transfers between devices with their start and end apart: 23 -> 15, of which waited for: 17 -> 11; matrix products, arithmetic and copies ran while one was open for 18% -> 15% of each run, Pallas kernels for 0% -> 0%
where the time goes in v1:
time: 556 us; the launch traced here: 552 us
  waiting for transfers between devices  344 us (62%)
  matrix products  65.1 us (12%)
  local copies, waits for them, and re-layouts  55.3 us (10%)
  other arithmetic  39 us (7%)
  blocking collectives  24.8 us (4%)
  between operations  16.9 us (3%)
  starting transfers between devices  7.27 us (1%)
    reduce_scatter x3, waiting for transfers between devices, scattered(): lax.psum_scatter(member.astype(jnp.bfloat16), axes, scatter_dimension=0,...  97.4 us
    psum x1, waiting for transfers between devices, local(): feed = lax.psum(feed_part.astype(jnp.bfloat16), 'tp').astype(jnp.float32)  43.7 us
    unnamed x12, waiting for transfers between devices  41.4 us
    psum x1, waiting for transfers between devices, local(): lax.psum(mixer_part.astype(jnp.bfloat16), 'tp').astype(jnp.float32)  37.4 us
    psum x1, waiting for transfers between devices, local(): lax.psum(two_part.astype(jnp.bfloat16), 'tp').astype(jnp.float32)  35.9 us
    all_gather x1, waiting for transfers between devices, local(): lax.all_gather(jnp.concatenate([query_weight, key_weight, value_weight, g...  32.6 us
    all_gather x1, waiting for transfers between devices, local(): lax.all_gather(jnp.concatenate([hidden_gate, hidden_up], 1), axes, axis=0...  32.4 us
    dot_general x33, matrix products, mm(): return jnp.einsum(spec, left, right, precision=HIGH)  25.1 us
  transfers between devices with their start and end apart: 15, of which 11 were waited for; matrix products, arithmetic and copies ran while one was open for 15% of the time, Pallas kernels for 0%

profile of v1, /device:TPU:0, one launch (start us, length us, event | category | flops | bytes accessed | tf_op | source)
XLA Modules:
  0.0 552.2 jit_solution(16827388496142749723)
XLA Ops:
  10.5 1.9 concatenate.50
  16.0 32.6 %all-gather.5.cloned.1.call-done = bf16[1024,1664]{1,0:T(8,128)(2,1)} async-done(((bf16[128,1664]{1,0:T(8,128)(2,1)}), bf16[1024,1664]{1,0:T(8,128)(2,1)}) %all-gather.5.cloned.1.call-update) | async-done | bytes 3407888 | tf_op jit(solution)/shard_map/all_gather | solution.py:223
  48.6 1.4 convert_reduce_fusion
  50.1 3.2 fusion.208
  53.3 2.6 collective-permute-start
  57.7 1.8 fusion.28
  80.3 1.3 convolution_add_fusion.14
  82.0 1.3 collective-permute-start.1
  89.1 1.9 multiply_convert_fusion.4
  91.0 2.6 convolution_convert_fusion.4
  95.2 37.4 %all-reduce.42.cloned.1.call-done = bf16[256,1024]{1,0:T(8,128)(2,1)} async-done(((bf16[256,1024]{1,0:T(8,128)(2,1)}), bf16[256,1024]{1,0:T(8,128)(2,1)}) %all-reduce.42.cloned.1.call-update) | async-done | bytes 524304 | tf_op jit(solution)/shard_map/psum | solution.py:278
  133.8 32.4 %all-gather.9.cloned.1.call-done = bf16[1024,1408]{0,1:T(8,128)(2,1)} async-done(((bf16[128,1408]{0,1:T(8,128)(2,1)}), bf16[1024,1408]{0,1:T(8,128)(2,1)}) %all-gather.9.cloned.1.call-update) | async-done | bytes 2883600 | tf_op jit(solution)/shard_map/all_gather | solution.py:243
  166.3 4.2 fusion.195
  170.5 22.7 %all-gather.11.cloned.1.call-done = bf16[1024,704]{0,1:T(8,128)(2,1)} async-done(((bf16[128,704]{0,1:T(8,128)(2,1)}), bf16[1024,704]{0,1:T(8,128)(2,1)}) %all-gather.11.cloned.1.call-update) | async-done | bytes 1441808 | tf_op jit(solution)/shard_map/all_gather | solution.py:246
  193.2 3.5 multiply_convert_fusion.2
  197.7 1.8 convolution_convert_fusion.5
  199.5 2.9 convolution_convert_fusion.6
  202.4 35.9 %all-reduce.44.cloned.1.call-done = bf16[256,1024]{1,0:T(8,128)(2,1)} async-done(((bf16[256,1024]{1,0:T(8,128)(2,1)}), bf16[256,1024]{1,0:T(8,128)(2,1)}) %all-reduce.44.cloned.1.call-update) | async-done | bytes 524304 | tf_op jit(solution)/shard_map/psum | solution.py:301
  238.3 2.3 fusion.17
  241.2 1.9 fusion.61
  243.9 2.1 fusion.41
  246.0 2.1 reshape.506
  248.1 2.2 reshape.507
  250.3 1.8 multiply_reduce_fusion.8
  253.5 2.1 convolution_add_fusion.13
  255.6 1.6 collective-permute-start.2
  263.1 1.5 copy.268
  265.3 1.9 fusion.48
  269.5 1.4 convolution_add_fusion.8
  273.4 1.3 convolution_bitcast_fusion.5
  281.8 1.4 multiply_reduce_fusion.10
  289.2 1.6 multiply_reduce_fusion.3
  294.5 1.6 fusion.199
  296.2 2.0 pad_add_fusion.3
  303.0 3.1 convolution_convert_fusion.3
  307.6 1.8 convolution_convert_fusion.2
  309.5 1.7 fusion.4
  311.1 2.6 copy.294
  314.9 2.7 convolution_convert_fusion
  317.7 43.7 %all-reduce.46.cloned.1.call-done = (bf16[256,1024]{1,0:T(8,128)(2,1)}, bf16[272,1024]{1,0:T(8,128)(2,1)}) async-done(((bf16[256,1024]{1,0:T(8,128)(2,1)}, bf16[272,1024]{1,0:T(8,128)(2,1)}), (bf16[256,1024]{1,0:T(8,128)(2,1)}, bf16[272,1024]{1,0:T(8,128)(2,1)})) %all-reduce.46.cloned.1.call-update) | async-done | bytes 1081360 | tf_op jit(solution)/shard_map/psum | solution.py:336
  363.2 3.1 select_convert_fusion
  367.7 24.8 %all-reduce.36 = (f32[4,1024]{1,0:T(4,128)S(1)}, f32[2]{0:T(128)}, f32[2]{0:T(128)}, f32[256]{0:T(256)}) all-reduce(f32[4,1024]{1,0:T(4,128)S(1)} %pad_add_fusion.15, f32[2]{0:T(128)S(1)} %negate_multiply_fusion, f32[2]{0:T(128)S(1)} %copy-done.148, f32[256]{0:T(256)S(1)} %bitcast.386), channel_id=1, replica_groups=mesh['dp'=4,'ctx'=2,'tp'=4] {'dp','ctx'}, use_global_device_ids=true, to_apply=%region_32.33 | all-reduce | flops 4356 | bytes 34848 | tf_op jit(solution)/shard_map/psum | solution.py:376
  393.6 2.9 fusion.25
  396.6 3.4 reduce-scatter.9.cloned.1.call-done
  400.0 1.6 convert_element_type.206
  401.6 40.0 %reduce-scatter.13.cloned.1.call-done = bf16[128,704]{1,0:T(8,128)(2,1)} async-done(((bf16[1024,704]{1,0:T(8,128)(2,1)}), bf16[128,704]{1,0:T(8,128)(2,1)}) %reduce-scatter.13.cloned.1.call-update) | async-done | bytes 180240
  443.5 46.1 %reduce-scatter.11.cloned.1.call-done = bf16[128,1408]{1,0:T(8,128)(2,1)} async-done(((bf16[1024,1408]{1,0:T(8,128)(2,1)}), bf16[128,1408]{1,0:T(8,128)(2,1)}) %reduce-scatter.11.cloned.1.call-update) | async-done | bytes 360464 | tf_op jit(solution)/shard_map/reduce_scatter | solution.py:355
  492.6 47.8 %reduce-scatter.7.cloned.1.call-done = bf16[128,1664]{1,0:T(8,128)(2,1)} async-done(((bf16[1024,1664]{1,0:T(8,128)(2,1)}), bf16[128,1664]{1,0:T(8,128)(2,1)}) %reduce-scatter.7.cloned.1.call-update) | async-done | bytes 426000 | tf_op jit(solution)/shard_map/reduce_scatter | solution.py:355
  (538 shorter events, 89.5 us)
Async XLA Ops:
  7.2 7.3 %copy-start.136 = (f32[256]{0:T(256)S(1)}, f32[256]{0:T(256)}, u32[]{:S(2)}) copy-start(f32[256]{0:T(256)} %param.40) | copy-start | bytes 3076
  7.2 7.9 %copy-start.150 = (s32[1,512]{1,0:T(1,128)S(1)}, s32[1,512]{1,0:T(1,128)}, u32[]{:S(2)}) copy-start(s32[1,512]{1,0:T(1,128)} %param.24) | copy-start | bytes 6148
  7.2 8.1 %copy-start = (bf16[1,256,1024]{2,1,0:T(8,128)(2,1)S(1)}, bf16[1,256,1024]{2,1,0:T(8,128)(2,1)}, u32[]{:S(2)}) copy-start(bf16[1,256,1024]{2,1,0:T(8,128)(2,1)} %param.23) | copy-start | bytes 1572868
  7.2 8.3 %copy-start.142 = (f32[4,256]{1,0:T(4,128)S(1)}, f32[4,256]{1,0:T(4,128)}, u32[]{:S(2)}) copy-start(f32[4,256]{1,0:T(4,128)} %param.35) | copy-start | bytes 12292
  7.2 8.3 %copy-start.143 = (f32[4,256]{1,0:T(4,128)S(1)}, f32[4,256]{1,0:T(4,128)}, u32[]{:S(2)}) copy-start(f32[4,256]{1,0:T(4,128)} %param.36) | copy-start | bytes 12292
  7.2 8.3 %copy-start.139 = (f32[4,512]{1,0:T(4,128)S(1)}, f32[4,512]{1,0:T(4,128)}, u32[]{:S(2)}) copy-start(f32[4,512]{1,0:T(4,128)} %param.37) | copy-start | bytes 24580
  7.3 8.3 %copy-start.156 = (f32[2]{0:T(128)S(1)}, f32[2]{0:T(128)}, u32[]{:S(2)}) copy-start(f32[2]{0:T(128)} %param.38) | copy-start | bytes 28
  7.3 41.4 %all-gather.5.cloned.1.call-start = ((), (), s32[]{:S(2)}) async-start(), calls=%async_computation.4 | async-start | bytes 3833856 | tf_op jit(solution)/shard_map/all_gather | solution.py:223
  12.5 78.6 %all-gather.7.cloned.1.call-start = ((), (), s32[]{:S(2)}) async-start(), calls=%async_computation.5 | async-start | bytes 1179648 | tf_op jit(solution)/shard_map/all_gather | solution.py:242
  13.2 119.3 %all-reduce.42.cloned.1.call-start = ((), (), s32[]{:S(2)}) async-start(), calls=%async_computation.6 | async-start | bytes 1048576 | tf_op jit(solution)/shard_map/psum | solution.py:278
  15.3 42.4 %copy-start.130 = (f32[256]{0:T(256)}, f32[256]{0:T(256)S(1)}, u32[]{:S(2)}) copy-start(f32[256]{0:T(256)S(1)} %get-tuple-element.212) | copy-start | bytes 3076
  15.3 42.4 %copy-start.132 = (f32[256]{0:T(256)}, f32[256]{0:T(256)S(1)}, u32[]{:S(2)}) copy-start(f32[256]{0:T(256)S(1)} %get-tuple-element.213) | copy-start | bytes 3076
  15.3 42.4 %copy-start.134 = (f32[256]{0:T(256)}, f32[256]{0:T(256)S(1)}, u32[]{:S(2)}) copy-start(f32[256]{0:T(256)S(1)} %get-tuple-element.214) | copy-start | bytes 3076
  15.5 37.7 %copy-start.123 = (f32[256]{0:T(256)}, f32[256]{0:T(256)S(1)}, u32[]{:S(2)}) copy-start(f32[256]{0:T(256)S(1)} %add_rsqrt_fusion.3) | copy-start | bytes 3076
  15.6 42.1 %copy-start.105 = (f32[1,1024]{1,0:T(1,128)}, f32[1,1024]{1,0:T(1,128)S(1)}, u32[]{:S(2)}) copy-start(f32[1,1024]{1,0:T(1,128)S(1)} %get-tuple-element.205) | copy-start | bytes 12292
  15.6 42.1 %copy-start.107 = (f32[1,1024]{1,0:T(1,128)}, f32[1,1024]{1,0:T(1,128)S(1)}, u32[]{:S(2)}) copy-start(f32[1,1024]{1,0:T(1,128)S(1)} %get-tuple-element.206) | copy-start | bytes 12292
  15.6 42.1 %copy-start.109 = (f32[1,1024]{1,0:T(1,128)}, f32[1,1024]{1,0:T(1,128)S(1)}, u32[]{:S(2)}) copy-start(f32[1,1024]{1,0:T(1,128)S(1)} %get-tuple-element.207) | copy-start | bytes 12292
  15.6 42.1 %copy-start.111 = (f32[1,1024]{1,0:T(1,128)}, f32[1,1024]{1,0:T(1,128)S(1)}, u32[]{:S(2)}) copy-start(f32[1,1024]{1,0:T(1,128)S(1)} %get-tuple-element.208) | copy-start | bytes 12292
  15.6 40.2 %copy-start.153 = (f32[2]{0:T(128)}, f32[2]{0:T(128)S(1)}, u32[]{:S(2)}) copy-start(f32[2]{0:T(128)S(1)} %exponential_negate_fusion) | copy-start | bytes 28
  50.0 5.9 %copy-start.151 = (f32[2]{0:T(128)S(1)}, f32[2]{0:T(128)}, u32[]{:S(2)}) copy-start(f32[2]{0:T(128)} %param.39) | copy-start | bytes 28
  53.3 4.2 collective-permute-start
  61.3 3.5 copy-start.42
  74.3 7.4 %copy-start.25 = (f32[2,128,256]{2,1,0:T(8,128)}, f32[2,128,256]{2,1,0:T(8,128)S(1)}, u32[]{:S(2)}) copy-start(f32[2,128,256]{2,1,0:T(8,128)S(1)} %slice_add_fusion.4) | copy-start | bytes 786436
  82.0 2.4 collective-permute-start.1
  86.2 4.9 copy-start.16
  93.7 72.6 %all-gather.9.cloned.1.call-start = ((), (), s32[]{:S(2)}) async-start(), calls=%async_computation.7 | async-start | bytes 3244032 | tf_op jit(solution)/shard_map/all_gather | solution.py:243
  94.5 98.7 %all-gather.11.cloned.1.call-start = ((), (), s32[]{:S(2)}) async-start(), calls=%async_computation.8 | async-start | bytes 1622016 | tf_op jit(solution)/shard_map/all_gather | solution.py:246
  95.1 143.2 %all-reduce.44.cloned.1.call-start = ((), (), s32[]{:S(2)}) async-start(), calls=%async_computation.9 | async-start | bytes 1048576 | tf_op jit(solution)/shard_map/psum | solution.py:301
  166.3 27.0 %copy-start.58 = (bf16[1,256,1024]{2,1,0:T(8,128)(2,1)S(1)}, bf16[1,256,1024]{2,1,0:T(8,128)(2,1)}, u32[]{:S(2)}) copy-start(bf16[1,256,1024]{2,1,0:T(8,128)(2,1)} %param.25) | copy-start | bytes 1572868
  193.2 4.4 copy-start.40
  199.5 38.9 %copy-start.1 = (bf16[256,1024]{1,0:T(8,128)(2,1)S(1)}, bf16[256,1024]{1,0:T(8,128)(2,1)}, u32[]{:S(2)}) copy-start(bf16[256,1024]{1,0:T(8,128)(2,1)} %all-reduce.42.cloned.1.call-done) | copy-start | bytes 1572868
  199.5 162.0 %all-reduce.46.cloned.1.call-start = ((), (), s32[]{:S(2)}) async-start(), calls=%async_computation.14 | async-start | bytes 2162688 | tf_op jit(solution)/shard_map/psum | solution.py:336
  253.1 4.2 copy-start.67
  253.1 4.2 copy-start.69
  253.1 4.2 copy-start.71
  253.5 3.8 copy-start.86
  253.5 4.8 copy-start.39
  253.5 4.7 copy-start.146
  255.6 11.7 %collective-permute-start.2 = (f32[2,128,256]{2,1,0:T(8,128)}, f32[2,128,256]{2,1,0:T(8,128)}, u32[]{:S(2)}, u32[]{:S(2)}) collective-permute-start(f32[2,128,256]{2,1,0:T(8,128)} %convolution_add_fusion.13), channel_id=1, source_target_pairs={{4,0},{5,1},{6,2},{7,3},{12,8},{13,9},{14,10},{15,11},{20,16},{21,... | collective-permute-start | bytes 786440 | tf_op jit(solution)/shard_map/ppermute | solution.py:20
  265.3 4.2 copy-start.5
  265.3 4.2 copy-start.122
  291.3 4.8 copy-start.117
  292.6 7.3 %collective-permute-start.3 = (f32[3,1024]{1,0:T(4,128)S(1)}, f32[3,1024]{1,0:T(4,128)S(1)}, u32[]{:S(2)}, u32[]{:S(2)}) collective-permute-start(f32[3,1024]{1,0:T(4,128)S(1)} %pad_add_fusion.14), channel_id=1, source_target_pairs={{4,0},{5,1},{6,2},{7,3},{12,8},{13,9},{14,10},{15,11},{20,16},{21,... | collective-permute-start | bytes 36872 | tf_op jit(solution)/shard_map/ppermute | solution.py:20
  307.0 92.9 %reduce-scatter.9.cloned.1.call-start = ((), (), s32[]{:S(2)}) async-start(), calls=%async_computation.11 | async-start | bytes 1179648 | tf_op jit(solution)/shard_map/reduce_scatter | solution.py:355
  309.4 132.3 %reduce-scatter.13.cloned.1.call-start = ((), (), s32[]{:S(2)}) async-start(), calls=%async_computation.13 | async-start | bytes 1769472
  313.8 175.8 %reduce-scatter.11.cloned.1.call-start = ((), (), s32[]{:S(2)}) async-start(), calls=%async_computation.12 | async-start | bytes 3244032 | tf_op jit(solution)/shard_map/reduce_scatter | solution.py:355
  317.6 45.1 %copy-start.124 = (f32[256]{0:T(256)S(1)}, f32[256]{0:T(256)}, u32[]{:S(2)}) copy-start(f32[256]{0:T(256)} %copy-done.123) | copy-start | bytes 3076
  317.6 222.8 %reduce-scatter.7.cloned.1.call-start = ((), (), s32[]{:S(2)}) async-start(), calls=%async_computation.10 | async-start | bytes 3833856 | tf_op jit(solution)/shard_map/reduce_scatter | solution.py:355
  (125 other events, 208.3 us)
Sparse Core Ops, SparseCore 0:
  12.6 35.9 all-gather.4
  50.5 23.3 all-gather.6
  93.8 38.6 all-reduce.41
  134.8 31.3 all-gather.8
  168.0 25.2 all-gather.10
  199.6 38.6 all-reduce.43
  307.2 54.2 all-reduce.45
  364.6 35.3 reduce-scatter.8
  403.3 38.3 reduce-scatter.12
  444.9 44.7 reduce-scatter.10
  493.1 47.2 reduce-scatter.6

commit v2 on v1

--- a/solution.py
+++ b/solution.py
@@ -3,6 +3,8 @@
 import jax
 import jax.numpy as jnp
 from jax import lax
+from jax.experimental import pallas as pl
+from jax.experimental.pallas import tpu as pltpu
 from jax.sharding import PartitionSpec as P
 
 GROUP = 64
@@ -12,6 +14,162 @@
 HIGHEST = lax.Precision.HIGHEST
 HIGH = lax.Precision.HIGH
 LANES = 128
+
+
+def peer_of(axes, sizes, distance):
+    flat = 0
+    total = 1
+    for axis, size in zip(axes, sizes):
+        flat = flat * size + lax.axis_index(axis)
+        total = total * size
+    other = lax.rem(flat + distance, total)
+    where = {}
+    for axis, size in reversed(list(zip(axes, sizes))):
+        where[axis] = lax.rem(other, size)
+        other = other // size
+    return where
+
+
+def greet(axes, sizes, peers):
+    barrier = pltpu.get_barrier_semaphore()
+    for distance in range(1, peers + 1):
+        pl.semaphore_signal(
+            barrier,
+            inc=1,
+            device_id=peer_of(axes, sizes, distance),
+            device_id_type=pl.DeviceIdType.MESH,
+        )
+    pl.semaphore_wait(barrier, peers)
+
+
+def sum_kernel(axis, size, x_ref, out_ref, parts, mine, got, send, recv, send_two, recv_two):
+    peers = size - 1
+    me = lax.axis_index(axis)
+    rows = x_ref.shape[0] // size
+    greet((axis,), (size,), peers)
+
+    def block(index):
+        return pl.ds(pl.multiple_of(index * rows, rows), rows)
+
+    copies = []
+    for distance in range(1, size):
+        other = lax.rem(me + distance, size)
+        copy = pltpu.make_async_remote_copy(
+            src_ref=x_ref.at[block(other)],
+            dst_ref=parts.at[distance - 1],
+            send_sem=send.at[distance - 1],
+            recv_sem=recv.at[distance - 1],
+            device_id={axis: other},
+            device_id_type=pl.DeviceIdType.MESH,
+        )
+        copy.start()
+        copies.append(copy)
+    total = x_ref[block(me)].astype(jnp.float32)
+    for distance in range(1, size):
+        copies[distance - 1].wait_recv()
+        total = total + parts[distance - 1].astype(jnp.float32)
+    total = total.astype(out_ref.dtype)
+    mine[...] = total
+    out_ref[block(me)] = total
+    more = []
+    for distance in range(1, size):
+        copy = pltpu.make_async_remote_copy(
+            src_ref=mine,
+            dst_ref=got.at[distance - 1],
+            send_sem=send_two.at[distance - 1],
+            recv_sem=recv_two.at[distance - 1],
+            device_id={axis: lax.rem(me + distance, size)},
+            device_id_type=pl.DeviceIdType.MESH,
+        )
+        copy.start()
+        more.append(copy)
+    for distance in range(1, size):
+        more[distance - 1].wait_recv()
+        out_ref[block(lax.rem(me + size - distance, size))] = got[distance - 1]
+    for copy in copies + more:
+        copy.wait_send()
+
+
+def summed(value, axis, call):
+    size = lax.axis_size(axis)
+    if size == 1:
+        return value
+    rows, cols = value.shape
+    piece = (size - 1, rows // size, cols)
+    sems = pltpu.SemaphoreType.DMA((size - 1,))
+    return pl.pallas_call(
+        partial(sum_kernel, axis, size),
+        out_shape=jax.ShapeDtypeStruct(value.shape, value.dtype),
+        in_specs=[pl.BlockSpec(memory_space=pltpu.VMEM)],
+        out_specs=pl.BlockSpec(memory_space=pltpu.VMEM),
+        scratch_shapes=[
+            pltpu.VMEM(piece, value.dtype),
+            pltpu.VMEM(piece[1:], value.dtype),
+            pltpu.VMEM(piece, value.dtype),
+            sems,
+            sems,
+            sems,
+            sems,
+        ],
+        cost_estimate=pl.CostEstimate(
+            flops=value.size * 40000, bytes_accessed=value.size * 300, transcendentals=0
+        ),
+        compiler_params=pltpu.CompilerParams(collective_id=call, has_side_effects=True),
+        name=f"tp_sum_{call}",
+    )(value)
+
+
+def small_kernel(axes, sizes, peers, x_ref, out_ref, parts, send, recv):
+    greet(axes, sizes, peers)
+    copies = []
+    for distance in range(1, peers + 1):
+        copy = pltpu.make_async_remote_copy(
+            src_ref=x_ref,
+            dst_ref=parts.at[distance - 1],
+            send_sem=send.at[distance - 1],
+            recv_sem=recv.at[distance - 1],
+            device_id=peer_of(axes, sizes, distance),
+            device_id_type=pl.DeviceIdType.MESH,
+        )
+        copy.start()
+        copies.append(copy)
+    flat = 0
+    for axis, size in zip(axes, sizes):
+        flat = flat * size + lax.axis_index(axis)
+    for copy in copies:
+        copy.wait()
+    parts[peers] = x_ref[...]
+    total = jnp.zeros(x_ref.shape, jnp.float32)
+    for owner in range(peers + 1):
+        slot = lax.rem(flat + 2 * (peers + 1) - owner - 1, peers + 1)
+        total = total + parts[slot]
+    out_ref[...] = total
+
+
+def small_sum(value, axes, call):
+    sizes = tuple(lax.axis_size(axis) for axis in axes)
+    peers = 1
+    for size in sizes:
+        peers = peers * size
+    peers = peers - 1
+    if peers == 0:
+        return value
+    return pl.pallas_call(
+        partial(small_kernel, axes, sizes, peers),
+        out_shape=jax.ShapeDtypeStruct(value.shape, value.dtype),
+        in_specs=[pl.BlockSpec(memory_space=pltpu.VMEM)],
+        out_specs=pl.BlockSpec(memory_space=pltpu.VMEM),
+        scratch_shapes=[
+            pltpu.VMEM((peers + 1,) + value.shape, value.dtype),
+            pltpu.SemaphoreType.DMA((peers,)),
+            pltpu.SemaphoreType.DMA((peers,)),
+        ],
+        cost_estimate=pl.CostEstimate(
+            flops=1000000, bytes_accessed=20000000, transcendentals=0
+        ),
+        compiler_params=pltpu.CompilerParams(collective_id=call, has_side_effects=True),
+        name=f"small_sum_{call}",
+    )(value)
 
 
 def passed_along(value, axis, by):
@@ -275,7 +433,7 @@
     mixed, finish_back = jax.vjp(finish, carried, local_out, initial, gate_lin, head_gain)
     mixed_b = mixed.astype(jnp.bfloat16)
     mixer_part = jnp.einsum("rc,dc->rd", mixed_b, full_output, preferred_element_type=jnp.float32)
-    attention = lax.psum(mixer_part.astype(jnp.bfloat16), "tp").astype(jnp.float32)
+    attention = summed(mixer_part.astype(jnp.bfloat16), "tp", 0).astype(jnp.float32)
     middle = inputs + attention
     rms_two = lax.rsqrt(jnp.mean(middle * middle, -1, keepdims=True) + EPSILON)
     normed_two = middle * rms_two
@@ -298,7 +456,19 @@
         "rd,rf->df", hidden_two, d_gate_up, preferred_element_type=jnp.float32
     )
     two_part = jnp.einsum("rf,df->rd", d_gate_up, full_gate_up, preferred_element_type=jnp.float32)
-    d_hidden_two = lax.psum(two_part.astype(jnp.bfloat16), "tp").astype(jnp.float32)
+    both = summed(jnp.concatenate([two_part, feed_part], 0).astype(jnp.bfloat16), "tp", 1)
+    d_hidden_two = both[:row_count].astype(jnp.float32)
+    feed = both[row_count:].astype(jnp.float32)
+    block_out = (middle + feed).astype(jnp.bfloat16).reshape(tokens.shape)
+
+    def scattered(member):
+        total = lax.psum_scatter(
+            member.astype(jnp.bfloat16), axes, scatter_dimension=0, tiled=True
+        )
+        return total.astype(jnp.float32)
+
+    down_own = scattered(grad_down)
+    gate_up_own = scattered(grad_gate_up)
     grad_gain_two = jnp.sum(d_hidden_two * normed_two, 0)
     dn_two = d_hidden_two * gain_two
     d_middle = grad_out + rms_two * (
@@ -327,14 +497,10 @@
     ).astype(jnp.bfloat16)
     grad_input = jnp.einsum("rd,rc->dc", hidden_one, d_proj, preferred_element_type=jnp.float32)
     one_part = jnp.einsum("rc,dc->rd", d_proj, in_weights, preferred_element_type=jnp.float32)
-    value_dim = d_head.shape[0]
-    head_row = jnp.zeros((16, width), jnp.bfloat16)
-    head_row = head_row.at[0, :value_dim].set(d_head.astype(jnp.bfloat16))
-    one_sum = lax.psum(jnp.concatenate([one_part.astype(jnp.bfloat16), head_row], 0), "tp")
-    one_sum = one_sum.astype(jnp.float32)
-    d_hidden_one, head_sum = one_sum[:row_count], one_sum[row_count, :value_dim]
-    feed = lax.psum(feed_part.astype(jnp.bfloat16), "tp").astype(jnp.float32)
-    block_out = (middle + feed).astype(jnp.bfloat16).reshape(tokens.shape)
+    one_part, down_own = lax.optimization_barrier((one_part, down_own))
+    one_sum = summed(one_part.astype(jnp.bfloat16), "tp", 2)
+    one_sum, gate_up_own = lax.optimization_barrier((one_sum, gate_up_own))
+    d_hidden_one = one_sum.astype(jnp.float32)
     grad_gain_one = jnp.sum(d_hidden_one * normed_one, 0)
     dn_one = d_hidden_one * gain_one
     tokens_grad = d_middle + rms_one * (
@@ -351,17 +517,9 @@
         conv_cols + value_cols + 2 * head_count,
     ]
 
-    def scattered(member):
-        total = lax.psum_scatter(
-            member.astype(jnp.bfloat16), axes, scatter_dimension=0, tiled=True
-        )
-        return total.astype(jnp.float32)
-
     column = jnp.arange(grad_input.shape[1])[None, :]
     grad_input = jnp.where(column == used - 2, grad_gain_one[:, None], grad_input)
     grad_input = jnp.where(column == used - 1, grad_gain_two[:, None], grad_input)
-    down_own = scattered(grad_down)
-    gate_up_own = scattered(grad_gate_up)
     output_own = scattered(grad_output)
     input_own = scattered(grad_input)
     reduced = (
@@ -373,9 +531,22 @@
         gate_up_own[:, ff_cols:],
         down_own,
     )
-    conv_total, log_total, bias_total, head_total = lax.psum(
-        (d_conv, d_log, d_bias, head_sum), ("dp", "ctx")
-    )
+    taps, conv_width = d_conv.shape
+    value_dim = d_head.shape[0]
+    rest = jnp.concatenate([d_head, d_log, d_bias])
+    pad_row = jnp.zeros((-rest.shape[0] % conv_width,), jnp.float32)
+    rest = jnp.concatenate([rest, pad_row]).reshape(-1, conv_width)
+    packed = jnp.concatenate([d_conv, rest], 0)
+    lines = packed.shape[0]
+    packed = jnp.concatenate([packed, jnp.zeros((-lines % 8, conv_width), jnp.float32)], 0)
+    packed = small_sum(packed, ("dp", "ctx"), 3)
+    conv_total = packed[:taps]
+    rest = packed[taps:lines].reshape(-1)
+    log_total = rest[value_dim : value_dim + head_count]
+    bias_total = rest[value_dim + head_count : value_dim + 2 * head_count]
+    head_total = small_sum(
+        jnp.broadcast_to(rest[None, :value_dim], (8, value_dim)), ("tp",), 4
+    )[0]
     return (
         block_out,
         tokens_grad,

time: 556 us -> 381 us (0.69)
  waiting for transfers between devices: 344 us -> 49.9 us
  Pallas kernels: 0 us -> 126 us
  blocking collectives: 24.8 us -> 0 us
  matrix products: 65.1 us -> 76.9 us
    pallas_call x0 -> x5, Pallas kernels: none -> 126 us  [the longest x3 108 us: summed(): pl.pallas_call(partial(sum_kernel, axis, size), out_shape=jax.ShapeDtypeS...]
    psum x3 -> x0, waiting for transfers between devices: 117 us -> none  [the longest x1 43.7 us: local(): feed = lax.psum(feed_part.astype(jnp.bfloat16), 'tp').astype(jnp.float32)]
    reduce_scatter x3, waiting for transfers between devices: 97.4 us -> 16.4 us  [scattered(): lax.psum_scatter(member.astype(jnp.bfloat16), axes, scatter_dimension=0,...]
    unnamed x12 -> x9, waiting for transfers between devices: 41.4 us -> 1.32 us
    all_gather x1, waiting for transfers between devices: 32.4 us -> 0.01 us  [local(): lax.all_gather(jnp.concatenate([hidden_gate, hidden_up], 1), axes, axis=0...]
    psum x1 -> x0, blocking collectives: 24.8 us -> none  [local(): lax.psum((d_conv, d_log, d_bias, head_sum), ('dp', 'ctx'))]
    all_gather x1, waiting for transfers between devices: 22.7 us -> 0.01 us  [local(): full_hidden_down = lax.all_gather(hidden_down, axes, axis=0, tiled=True)]
    dot_general x33, matrix products: 25.1 us -> 35.9 us  [mm(): return jnp.einsum(spec, left, right, precision=HIGH)]
  transfers between devices with their start and end apart: 15 -> 12, of which waited for: 11 -> 3; matrix products, arithmetic and copies ran while one was open for 15% -> 40% of each run, Pallas kernels for 0% -> 33%
where the time goes in v2:
time: 381 us; the launch traced here: 377 us
  Pallas kernels  126 us (33%)
  matrix products  76.9 us (20%)
  local copies, waits for them, and re-layouts  58.6 us (15%)
  waiting for transfers between devices  49.9 us (13%)
  other arithmetic  41.5 us (11%)
  between operations  16.8 us (4%)
  starting transfers between devices  7.23 us (2%)
    pallas_call x3, Pallas kernels, summed(): pl.pallas_call(partial(sum_kernel, axis, size), out_shape=jax.ShapeDtypeS...  108 us
    dot_general x33, matrix products, mm(): return jnp.einsum(spec, left, right, precision=HIGH)  35.9 us
    all_gather x1, waiting for transfers between devices, local(): lax.all_gather(jnp.concatenate([query_weight, key_weight, value_weight, g...  31.8 us
    unnamed x317, local copies, waits for them, and re-layouts  21.7 us
    pallas_call x2, Pallas kernels, small_sum(): pl.pallas_call(partial(small_kernel, axes, sizes, peers), out_shape=jax.S...  18.1 us
    reduce_scatter x3, waiting for transfers between devices, scattered(): lax.psum_scatter(member.astype(jnp.bfloat16), axes, scatter_dimension=0,...  16.4 us
  transfers between devices with their start and end apart: 12, of which 3 were waited for; matrix products, arithmetic and copies ran while one was open for 40% of the time, Pallas kernels for 33%

profile of v2, /device:TPU:0, one launch (start us, length us, event | category | flops | bytes accessed | tf_op | source)
XLA Modules:
  0.0 377.4 jit_solution(6367647556279300567)
XLA Ops:
  10.6 1.9 concatenate.55
  16.9 31.8 %all-gather.5.cloned.1.call-done = bf16[1024,1664]{1,0:T(8,128)(2,1)} async-done(((bf16[128,1664]{1,0:T(8,128)(2,1)}), bf16[1024,1664]{1,0:T(8,128)(2,1)}) %all-gather.5.cloned.1.call-update) | async-done | bytes 3407888 | tf_op jit(solution)/shard_map/all_gather | solution.py:381
  48.7 1.4 convert_reduce_fusion
  50.2 3.2 fusion.206
  53.4 2.5 collective-permute-start
  57.4 1.8 fusion.27
  78.3 12.5 %convolution_add_fusion.14 = f32[2,128,256]{2,1,0:T(8,128)S(1)} fusion(f32[8,128,384]{2,1,0:T(8,128)} %copy-done.12, f32[2,128,384]{2,1,0:T(8,128)} %fusion.63), kind=kOutput, calls=%fused_computation.48 | convolution fusion | flops 50462720 | bytes 917504 | tf_op jit(solution)/shard_map/hde,hew->hdw/dot_general | solution.py:245
  90.9 1.4 collective-permute-start.1
  98.1 1.9 multiply_convert_fusion.4
  100.0 2.6 convolution_convert_fusion.3.x_ref
  102.6 26.5 %tp_sum_0.1 = bf16[256,1024]{1,0:T(8,128)(2,1)} custom-call(bf16[256,1024]{1,0:T(8,128)(2,1)} %convolution_convert_fusion.3.x_ref), custom_call_target="tpu_custom_call" | custom-call | flops 10485760000 | bytes 78643200 | tf_op jit(solution)/shard_map/tp_sum_0/pallas_call | solution.py:100
  131.0 4.3 %fusion.193 = f32[256,1408]{0,1:T(8,128)} fusion(bf16[1024,1408]{0,1:T(8,128)(2,1)} %all-gather.11.cloned.1.call-done, bf16[256,1024]{1,0:T(8,128)(2,1)} %tp_sum_0.1, bf16[1,256,1024]{2,1,0:T(8,128)(2,1)S(1)} %copy-done, f32[1024]{0:T(1024)S(1)} %get-tuple-element.128, f32[256]{0:T(256)} %add_rsqrt_fusion.2), kind=kOutput, calls=%fused_computation.363 | convolution fusion | flops 739770368 | bytes 5379072 | tf_op jit(solution)/shard_map/dot_general | solution.py:441
  135.2 3.4 multiply_convert_fusion.3
  139.4 1.7 fusion.4
  141.1 2.6 copy.294
  143.8 3.8 %convolution_convert_fusion = bf16[1024,1408]{1,0:T(8,128)(2,1)} fusion(bf16[256,704]{0,1:T(8,128)(2,1)} %get-tuple-element.157, bf16[256,704]{0,1:T(8,128)(2,1)} %get-tuple-element.156, bf16[256,1024]{1,0:T(8,128)(2,1)S(1)} %copy-done.3, bf16[1,256,1024]{2,1,0:T(8,128)(2,1)S(1)} %copy-done, f32[1024]{0:T(1024)S(1)} %get-tuple-element.128, ...), kind=kOutput, calls=%fused_computation.1 | convolution fusion | flops 742653952 | bytes 4658176 | tf_op jit(solution)/shard_map/rd,rf->df/dot_general | solution.py:455
  147.6 3.2 convolution_convert_fusion.4
  152.6 49.1 %tp_sum_1.1 = bf16[512,1024]{1,0:T(8,128)(2,1)} custom-call(bf16[512,1024]{1,0:T(8,128)(2,1)} %pad_maximum_fusion.1.x_ref), custom_call_target="tpu_custom_call" | custom-call | flops 20971520000 | bytes 157286400 | tf_op jit(solution)/shard_map/tp_sum_1/pallas_call | solution.py:100
  201.7 2.3 fusion.20
  204.6 2.7 fusion.59
  207.3 2.2 reshape.480
  209.4 2.6 fusion.39
  212.0 2.2 reshape.481
  214.2 2.5 multiply_reduce_fusion.6
  218.2 1.9 convolution_add_fusion.13
  225.6 1.9 convolution_convert_fusion.2
  228.1 1.9 copy.264
  230.0 1.5 copy.268
  231.5 1.5 copy.265
  233.5 1.9 fusion.46
  237.7 1.4 convolution_add_fusion.8
  241.5 1.3 convolution_bitcast_fusion.5
  250.1 1.4 multiply_reduce_fusion.10
  257.3 1.6 multiply_reduce_fusion.3
  263.7 2.1 pad_add_fusion.3
  269.7 3.9 %fusion.215.x_ref = bf16[256,1024]{1,0:T(8,128)(2,1)} fusion(bf16[256,1664]{1,0:T(8,128)(2,1)S(1)} %concatenate.68, bf16[1024,1664]{1,0:T(8,128)(2,1)} %all-gather.5.cloned.1.call-done), kind=kOutput, calls=%fused_computation.381 | convolution fusion | flops 872415232 | bytes 4784128 | tf_op jit(solution)/shard_map/rc,dc->rd/dot_general | solution.py:499
  275.4 32.6 %tp_sum_2.1 = bf16[256,1024]{1,0:T(8,128)(2,1)} custom-call(bf16[256,1024]{1,0:T(8,128)(2,1)} %fusion.215.x_ref), custom_call_target="tpu_custom_call" | custom-call | flops 10485760000 | bytes 78643200 | tf_op jit(solution)/shard_map/tp_sum_2/pallas_call | solution.py:100
  309.1 1.5 fusion.25
  310.7 3.0 select_convert_fusion
  315.2 7.9 %small_sum_3.1 = f32[8,1024]{1,0:T(8,128)} custom-call(f32[8,1024]{1,0:T(8,128)} %maximum_maximum_fusion.x_ref), custom_call_target="tpu_custom_call" | custom-call | flops 1000000 | bytes 20000000 | tf_op jit(solution)/shard_map/small_sum_3/pallas_call | solution.py:157
  325.7 10.3 %small_sum_4.1 = f32[8,256]{1,0:T(8,128)} custom-call(f32[8,256]{1,0:T(8,128)} %broadcast_in_dim.173.x_ref), custom_call_target="tpu_custom_call" | custom-call | flops 1000000 | bytes 20000000 | tf_op jit(solution)/shard_map/small_sum_4/pallas_call | solution.py:157
  337.2 1.3 slice_bitcast_fusion.7
  338.6 1.3 fusion.204
  339.9 1.6 convert_element_type.191
  342.5 2.0 copy.276
  344.5 1.9 copy.277
  346.5 1.9 fusion.16
  348.4 16.3 %reduce-scatter.9.cloned.1.call-done = bf16[128,1664]{1,0:T(8,128)(2,1)} async-done(((bf16[1024,1664]{1,0:T(8,128)(2,1)}), bf16[128,1664]{1,0:T(8,128)(2,1)}) %reduce-scatter.9.cloned.1.call-update) | async-done | bytes 426000 | tf_op jit(solution)/shard_map/reduce_scatter | solution.py:465
  (524 shorter events, 86.5 us)
Async XLA Ops:
  7.2 6.2 %copy-start.89 = (bf16[128,704]{0,1:T(8,128)(2,1)S(1)}, bf16[128,704]{0,1:T(8,128)(2,1)}, u32[]{:S(2)}) copy-start(bf16[128,704]{0,1:T(8,128)(2,1)} %param.40) | copy-start | bytes 540676
  7.2 6.2 %copy-start.90 = (bf16[128,704]{0,1:T(8,128)(2,1)S(1)}, bf16[128,704]{0,1:T(8,128)(2,1)}, u32[]{:S(2)}) copy-start(bf16[128,704]{0,1:T(8,128)(2,1)} %param.39) | copy-start | bytes 540676
  7.2 8.2 %copy-start = (bf16[1,256,1024]{2,1,0:T(8,128)(2,1)S(1)}, bf16[1,256,1024]{2,1,0:T(8,128)(2,1)}, u32[]{:S(2)}) copy-start(bf16[1,256,1024]{2,1,0:T(8,128)(2,1)} %param.21) | copy-start | bytes 1572868
  7.2 41.5 %all-gather.5.cloned.1.call-start = ((), (), s32[]{:S(2)}) async-start(), calls=%async_computation.4 | async-start | bytes 3833856 | tf_op jit(solution)/shard_map/all_gather | solution.py:381
  10.5 5.1 %copy-start.140 = (s32[1,512]{1,0:T(1,128)S(1)}, s32[1,512]{1,0:T(1,128)}, u32[]{:S(2)}) copy-start(s32[1,512]{1,0:T(1,128)} %param.22) | copy-start | bytes 6148
  10.5 5.3 %copy-start.131 = (f32[4,256]{1,0:T(4,128)S(1)}, f32[4,256]{1,0:T(4,128)}, u32[]{:S(2)}) copy-start(f32[4,256]{1,0:T(4,128)} %param.33) | copy-start | bytes 12292
  10.5 5.3 %copy-start.132 = (f32[4,256]{1,0:T(4,128)S(1)}, f32[4,256]{1,0:T(4,128)}, u32[]{:S(2)}) copy-start(f32[4,256]{1,0:T(4,128)} %param.34) | copy-start | bytes 12292
  10.6 5.3 %copy-start.129 = (f32[4,512]{1,0:T(4,128)S(1)}, f32[4,512]{1,0:T(4,128)}, u32[]{:S(2)}) copy-start(f32[4,512]{1,0:T(4,128)} %param.35) | copy-start | bytes 24580
  10.6 5.5 %copy-start.148 = (f32[2]{0:T(128)S(1)}, f32[2]{0:T(128)}, u32[]{:S(2)}) copy-start(f32[2]{0:T(128)} %param.36) | copy-start | bytes 28
  10.6 5.5 %copy-start.126 = (f32[256]{0:T(256)S(1)}, f32[256]{0:T(256)}, u32[]{:S(2)}) copy-start(f32[256]{0:T(256)} %param.38) | copy-start | bytes 3076
  12.5 87.5 %all-gather.7.cloned.1.call-start = ((), (), s32[]{:S(2)}) async-start(), calls=%async_computation.5 | async-start | bytes 1179648 | tf_op jit(solution)/shard_map/all_gather | solution.py:400
  13.3 117.7 %all-gather.11.cloned.1.call-start = ((), (), s32[]{:S(2)}) async-start(), calls=%async_computation.7 | async-start | bytes 3244032 | tf_op jit(solution)/shard_map/all_gather | solution.py:401
  14.1 121.1 %all-gather.9.cloned.1.call-start = ((), (), s32[]{:S(2)}) async-start(), calls=%async_computation.6 | async-start | bytes 1622016 | tf_op jit(solution)/shard_map/all_gather | solution.py:404
  14.7 258.8 %reduce-scatter.13.cloned.1.call-start = ((), (), s32[]{:S(2)}) async-start(), calls=%async_computation.11 | async-start | bytes 1769472
  14.8 51.9 %copy-start.91 = (f32[64,64]{1,0:T(8,128)}, f32[64,64]{1,0:T(8,128)S(1)}, u32[]{:S(2)}) copy-start(f32[64,64]{1,0:T(8,128)S(1)} %get-tuple-element.215) | copy-start | bytes 49156
  15.6 37.7 %copy-start.124 = (f32[256]{0:T(256)}, f32[256]{0:T(256)S(1)}, u32[]{:S(2)}) copy-start(f32[256]{0:T(256)S(1)} %add_rsqrt_fusion.3) | copy-start | bytes 3076
  15.8 41.5 %copy-start.118 = (f32[256]{0:T(256)}, f32[256]{0:T(256)S(1)}, u32[]{:S(2)}) copy-start(f32[256]{0:T(256)S(1)} %get-tuple-element.204) | copy-start | bytes 3076
  15.8 41.5 %copy-start.120 = (f32[256]{0:T(256)}, f32[256]{0:T(256)S(1)}, u32[]{:S(2)}) copy-start(f32[256]{0:T(256)S(1)} %get-tuple-element.205) | copy-start | bytes 3076
  15.8 41.5 %copy-start.122 = (f32[256]{0:T(256)}, f32[256]{0:T(256)S(1)}, u32[]{:S(2)}) copy-start(f32[256]{0:T(256)S(1)} %get-tuple-element.206) | copy-start | bytes 3076
  15.9 41.4 %copy-start.95 = (f32[1,1024]{1,0:T(1,128)}, f32[1,1024]{1,0:T(1,128)S(1)}, u32[]{:S(2)}) copy-start(f32[1,1024]{1,0:T(1,128)S(1)} %get-tuple-element.197) | copy-start | bytes 12292
  15.9 41.4 %copy-start.97 = (f32[1,1024]{1,0:T(1,128)}, f32[1,1024]{1,0:T(1,128)S(1)}, u32[]{:S(2)}) copy-start(f32[1,1024]{1,0:T(1,128)S(1)} %get-tuple-element.198) | copy-start | bytes 12292
  15.9 41.4 %copy-start.99 = (f32[1,1024]{1,0:T(1,128)}, f32[1,1024]{1,0:T(1,128)S(1)}, u32[]{:S(2)}) copy-start(f32[1,1024]{1,0:T(1,128)S(1)} %get-tuple-element.199) | copy-start | bytes 12292
  16.0 41.4 %copy-start.101 = (f32[1,1024]{1,0:T(1,128)}, f32[1,1024]{1,0:T(1,128)S(1)}, u32[]{:S(2)}) copy-start(f32[1,1024]{1,0:T(1,128)S(1)} %get-tuple-element.200) | copy-start | bytes 12292
  16.1 39.8 %copy-start.145 = (f32[2]{0:T(128)}, f32[2]{0:T(128)S(1)}, u32[]{:S(2)}) copy-start(f32[2]{0:T(128)S(1)} %exponential_negate_fusion) | copy-start | bytes 28
  50.2 5.8 %copy-start.143 = (f32[2]{0:T(128)S(1)}, f32[2]{0:T(128)}, u32[]{:S(2)}) copy-start(f32[2]{0:T(128)} %param.37) | copy-start | bytes 28
  53.4 3.8 %collective-permute-start = (bf16[3,1024]{1,0:T(4,128)(2,1)S(1)}, bf16[3,1024]{1,0:T(4,128)(2,1)S(1)}, u32[]{:S(2)}, u32[]{:S(2)}) collective-permute-start(bf16[3,1024]{1,0:T(4,128)(2,1)S(1)} %slice.344), channel_id=1, source_target_pairs={{0,4},{1,5},{2,6},{3,7},{8,12},{9,13},{10,14},{11,15},{16,20},{17,... | collective-permute-start | bytes 18440 | tf_op jit(solution)/shard_map/ppermute | solution.py:178
  65.0 5.1 %copy-start.6 = (f32[4,2,64,256]{3,2,1,0:T(8,128)}, f32[4,2,64,256]{3,2,1,0:T(8,128)S(1)}, u32[]{:S(2)}) copy-start(f32[4,2,64,256]{3,2,1,0:T(8,128)S(1)} %copy.238) | copy-start | bytes 1572868
  65.1 5.0 %copy-start.19 = (f32[8,64,128]{2,1,0:T(8,128)}, f32[8,64,128]{2,1,0:T(8,128)S(1)}, u32[]{:S(2)}) copy-start(f32[8,64,128]{2,1,0:T(8,128)S(1)} %broadcast_multiply_fusion.2) | copy-start | bytes 786436
  77.5 14.8 %copy-start.64 = (f32[1,2,128,384]{3,2,1,0:T(8,128)S(1)}, f32[1,2,128,384]{3,2,1,0:T(8,128)}, u32[]{:S(2)}) copy-start(f32[1,2,128,384]{3,2,1,0:T(8,128)} %fusion.66) | copy-start | bytes 1179652
  77.5 14.8 %copy-start.66 = (f32[1,2,128,384]{3,2,1,0:T(8,128)S(1)}, f32[1,2,128,384]{3,2,1,0:T(8,128)}, u32[]{:S(2)}) copy-start(f32[1,2,128,384]{3,2,1,0:T(8,128)} %fusion.68) | copy-start | bytes 1179652
  77.5 14.8 %copy-start.68 = (f32[1,2,128,384]{3,2,1,0:T(8,128)S(1)}, f32[1,2,128,384]{3,2,1,0:T(8,128)}, u32[]{:S(2)}) copy-start(f32[1,2,128,384]{3,2,1,0:T(8,128)} %fusion.64) | copy-start | bytes 1179652
  78.3 14.5 %copy-start.63 = (f32[6,64,128]{2,1,0:T(8,128)}, f32[6,64,128]{2,1,0:T(8,128)S(1)}, u32[]{:S(2)}) copy-start(f32[6,64,128]{2,1,0:T(8,128)S(1)} %slice.361) | copy-start | bytes 589828
  90.9 2.6 collective-permute-start.1
  95.1 4.9 %copy-start.16 = (f32[32,8,2,256]{3,1,2,0:T(8,128)}, f32[32,8,2,256]{3,1,2,0:T(8,128)S(1)}, u32[]{:S(2)}) copy-start(f32[32,8,2,256]{3,1,2,0:T(8,128)S(1)} %copy.299) | copy-start | bytes 1572868
  131.0 4.3 %copy-start.57 = (bf16[1,256,1024]{2,1,0:T(8,128)(2,1)S(1)}, bf16[1,256,1024]{2,1,0:T(8,128)(2,1)}, u32[]{:S(2)}) copy-start(bf16[1,256,1024]{2,1,0:T(8,128)(2,1)} %param.23) | copy-start | bytes 1572868
  143.7 164.3 %reduce-scatter.7.cloned.1.call-start = ((), (), s32[]{:S(2)}) async-start(), calls=%async_computation.8 | async-start | bytes 3244032 | tf_op jit(solution)/shard_map/reduce_scatter | solution.py:465
  201.7 138.3 %reduce-scatter.11.cloned.1.call-start = ((), (), s32[]{:S(2)}) async-start(), calls=%async_computation.10 | async-start | bytes 1179648 | tf_op jit(solution)/shard_map/reduce_scatter | solution.py:465
  217.4 5.0 %copy-start.81 = (f32[3,2,64,128]{3,2,1,0:T(8,128)}, f32[3,2,64,128]{3,2,1,0:T(8,128)S(1)}, u32[]{:S(2)}) copy-start(f32[3,2,64,128]{3,2,1,0:T(8,128)S(1)} %split.44) | copy-start | bytes 589828
  217.7 5.6 %copy-start.36 = (f32[3,2,64,256]{3,2,1,0:T(8,128)}, f32[3,2,64,256]{3,2,1,0:T(8,128)S(1)}, u32[]{:S(2)}) copy-start(f32[3,2,64,256]{3,2,1,0:T(8,128)S(1)} %split.43) | copy-start | bytes 1179652
  218.2 4.2 %copy-start.38 = (f32[4,64,2,128]{3,2,1,0:T(2,128)S(1)}, f32[4,64,2,128]{3,2,1,0:T(2,128)}, u32[]{:S(2)}) copy-start(f32[4,64,2,128]{3,2,1,0:T(2,128)} %reshape.466) | copy-start | bytes 786436
  220.1 15.3 %collective-permute-start.2 = (f32[2,128,256]{2,1,0:T(8,128)}, f32[2,128,256]{2,1,0:T(8,128)}, u32[]{:S(2)}, u32[]{:S(2)}) collective-permute-start(f32[2,128,256]{2,1,0:T(8,128)} %convolution_add_fusion.13), channel_id=1, source_target_pairs={{4,0},{5,1},{6,2},{7,3},{12,8},{13,9},{14,10},{15,11},{20,16},{21,... | collective-permute-start | bytes 786440 | tf_op jit(solution)/shard_map/ppermute | solution.py:178
  233.0 4.7 %copy-start.112 = (pred[384]{0:T(512)(128)(4,1)S(1)}, pred[384]{0:T(512)(128)(4,1)}, u32[]{:S(2)}) copy-start(pred[384]{0:T(512)(128)(4,1)} %constant.71.clone.1) | copy-start | bytes 1156
  233.0 131.7 %reduce-scatter.9.cloned.1.call-start = ((), (), s32[]{:S(2)}) async-start(), calls=%async_computation.9 | async-start | bytes 3833856 | tf_op jit(solution)/shard_map/reduce_scatter | solution.py:465
  259.3 4.3 %copy-start.108 = (f32[256,2]{0,1:T(2,128)S(1)}, f32[256,2]{0,1:T(2,128)}, u32[]{:S(2)}) copy-start(f32[256,2]{0,1:T(2,128)} %copy-done.107) | copy-start | bytes 6148
  260.6 6.9 %collective-permute-start.3 = (f32[3,1024]{1,0:T(4,128)S(1)}, f32[3,1024]{1,0:T(4,128)S(1)}, u32[]{:S(2)}, u32[]{:S(2)}) collective-permute-start(f32[3,1024]{1,0:T(4,128)S(1)} %pad_add_fusion.14), channel_id=1, source_target_pairs={{4,0},{5,1},{6,2},{7,3},{12,8},{13,9},{14,10},{15,11},{20,16},{21,... | collective-permute-start | bytes 36872 | tf_op jit(solution)/shard_map/ppermute | solution.py:178
  275.4 33.7 %copy-start.125 = (f32[256]{0:T(256)S(1)}, f32[256]{0:T(256)}, u32[]{:S(2)}) copy-start(f32[256]{0:T(256)} %copy-done.124) | copy-start | bytes 3076
  341.5 4.9 %copy-start.43 = (bf16[512,1024]{1,0:T(8,128)(2,1)S(1)}, bf16[512,1024]{1,0:T(8,128)(2,1)}, u32[]{:S(2)}) copy-start(bf16[512,1024]{1,0:T(8,128)(2,1)} %tp_sum_1.1) | copy-start | bytes 3145732
  341.5 4.9 %copy-start.137 = (f32[256]{0:T(256)S(1)}, f32[256]{0:T(256)}, u32[]{:S(2)}) copy-start(f32[256]{0:T(256)} %copy-done.135) | copy-start | bytes 3076
  (114 other events, 213.3 us)
Sparse Core Ops, SparseCore 0:
  12.7 35.9 all-gather.4
  50.6 23.3 all-gather.6
  76.5 31.5 all-gather.10
  109.8 25.1 all-gather.8
  143.8 41.6 reduce-scatter.12
  201.8 50.8 reduce-scatter.6
  255.8 35.9 reduce-scatter.10
  313.9 50.8 reduce-scatter.8
